TPU v7x, 512 devices: a whole 4x8x8 slice. The times are simulated.
512 devices in a mesh: dp: 16 (over x, z_hi, core), ctx: 32 (over z_lo, y).
Axes of the slice: x: 4, y: 8, z: 8 (z_hi: 2, z_lo: 4; z = z_hi * 4 + z_lo), core: 2. Of those that a mesh axis runs over, the one named last changes fastest.
Arguments:
- queries: bfloat16 [16, 4096, 1024], P('dp', 'ctx'), may hold values from -1.75 to 1.75
- keys: bfloat16 [16, 4096, 1024], P('dp', 'ctx'), may hold values from -1.8 to 1.8
- values: bfloat16 [16, 4096, 1024], P('dp', 'ctx'), may hold values from -3 to 3
- out_grad: bfloat16 [16, 4096, 1024], P('dp', 'ctx'), may hold values from -1.5 to 1.5
- layer_grad: bfloat16 [16, 4096, 768], P('dp', 'ctx'), may hold values from -6 to 6
- norm_gain: float32 [1024], replicated, may hold values from 0.1 to 1.9
- decay_rates: float32 [8], replicated, as said below
- doc_lengths: int32 [16, 4], P('dp'), may hold values from 1 to 2048, 4096 in all within a row
Outputs:
- query_grad: bfloat16 [16, 4096, 1024], P('dp', 'ctx')
- key_grad: bfloat16 [16, 4096, 1024], P('dp', 'ctx')
- value_grad: bfloat16 [16, 4096, 1024], P('dp', 'ctx')
- proj_grad: float32 [1024, 768], P(('dp', 'ctx'))
Inputs may be any that keep to these rules, and one draw needn't show every extreme that they name: `decay_rates`: positive rates; a head's state is multiplied by exp(-rate) per position. `doc_lengths`: each row sums to 4096; the longest document has exactly 2048 positions.
All inputs are finite; a program needn't handle non-finite values.
Results may differ from a plain program's by a relative error of at most 0.0029.
Values sent between devices are 32-bit elements; how exact they have to be, the bound alone decides.
A program may use at most 128 MiB of HBM per device.

v0:
```python
import math

import jax
import jax.numpy as jnp
from jax import lax
from jax.sharding import PartitionSpec as P

highest = lax.Precision.HIGHEST
norm_eps = 1e-06


def carried_in(value, axis, combine, identity, reverse):
    devices, here = (lax.axis_size(axis), lax.axis_index(axis))
    everything = jax.tree.map(lambda part: lax.all_gather(part, axis), value)
    start = jax.tree.map(
        lambda part, zero: jnp.broadcast_to(jnp.asarray(zero, part.dtype), part.shape),
        value,
        identity,
    )

    def lap(k, before):
        at = devices - 1 - k if reverse else k
        reached = at > here if reverse else at < here
        new = combine(before, jax.tree.map(lambda part: part[at], everything))
        return jax.tree.map(lambda a, b: jnp.where(reached, a, b), new, before)

    return lax.fori_loop(0, devices, lap, start)


def doc_index(positions, lengths):
    bounds = jnp.cumsum(lengths)[:-1]
    return jnp.sum((positions[..., None] >= bounds).astype(jnp.int32), axis=-1)


def decay_tables(decay_rate, doc_ids, prev_id, last_id):
    length = doc_ids.shape[0]
    offsets = jnp.arange(length, dtype=jnp.float32)
    distance = offsets[:, None] - offsets[None, :]
    same_doc = (doc_ids[:, None] == doc_ids[None, :]) & (distance >= 0.0)
    decay_mask = jnp.where(
        same_doc[None], jnp.exp(-decay_rate[:, None, None] * jnp.maximum(distance, 0.0)[None]), 0.0
    )
    entry_decay = jnp.where(
        (doc_ids == prev_id)[None, :], jnp.exp(-decay_rate[:, None] * offsets[None, :]), 0.0
    )
    exit_decay = jnp.where(
        (doc_ids == last_id)[None, :],
        jnp.exp(-decay_rate[:, None] * (length - offsets)[None, :]),
        0.0,
    )
    carry_all = jnp.where(last_id == prev_id, jnp.exp(-decay_rate * length), 0.0)
    return (decay_mask, entry_decay, exit_decay, carry_all)


def block_summary(query_rows, key_rows, value_rows, grad_rows, tables):
    decay_mask, entry_decay, exit_decay, carry_all = tables
    keys_out = key_rows * exit_decay.T[:, :, None]
    local_state = jnp.einsum("jhd,jhe->hde", keys_out, value_rows, precision=highest)
    queries_in = query_rows * entry_decay.T[:, :, None]
    state_pull = jnp.einsum("ihd,ihe->hde", queries_in, grad_rows, precision=highest)
    return (carry_all, local_state, state_pull)


def block_outputs(query_rows, key_rows, value_rows, grad_rows, tables, state_in, state_grad):
    decay_mask, entry_decay, exit_decay, carry_all = tables
    entry_t = entry_decay.T[:, :, None]
    exit_t = exit_decay.T[:, :, None]
    scores = jnp.einsum("ihd,jhd->hij", query_rows, key_rows, precision=highest) * decay_mask
    attention = jnp.einsum("hij,jhe->ihe", scores, value_rows, precision=highest)
    attention = attention + entry_t * jnp.einsum(
        "ihd,hde->ihe", query_rows, state_in, precision=highest
    )
    grads = jnp.einsum("ihe,jhe->hij", grad_rows, value_rows, precision=highest) * decay_mask
    query_grad = jnp.einsum("hij,jhd->ihd", grads, key_rows, precision=highest)
    query_grad = query_grad + entry_t * jnp.einsum(
        "ihe,hde->ihd", grad_rows, state_in, precision=highest
    )
    key_grad = jnp.einsum("hij,ihd->jhd", grads, query_rows, precision=highest)
    key_grad = key_grad + exit_t * jnp.einsum(
        "jhe,hde->jhd", value_rows, state_grad, precision=highest
    )
    value_grad = jnp.einsum("hij,ihe->jhe", scores, grad_rows, precision=highest)
    value_grad = value_grad + exit_t * jnp.einsum(
        "jhd,hde->jhe", key_rows, state_grad, precision=highest
    )
    return (attention, query_grad, key_grad, value_grad)


def compose(earlier, later):
    return (earlier[0] * later[0], later[0][..., None, None] * earlier[1] + later[1])


def on_device(queries, keys, values, out_grad, layer_grad, norm_gain, decay_rates, doc_lengths):
    seq_count, block_len, features = queries.shape
    head_count = decay_rates.shape[0]
    head_width = features // head_count
    ctx_index = lax.axis_index("ctx")
    positions = ctx_index * block_len + jnp.arange(block_len, dtype=jnp.int32)
    doc_ids = jax.vmap(doc_index, in_axes=(None, 0))(positions, doc_lengths)
    prev_ids = jax.vmap(doc_index, in_axes=(None, 0))(ctx_index * block_len - 1, doc_lengths)
    last_ids = doc_ids[:, -1]
    tables = jax.vmap(decay_tables, in_axes=(None, 0, 0, 0))(
        decay_rates, doc_ids, prev_ids, last_ids
    )

    def split_heads(array):
        return array.astype(jnp.float32).reshape(seq_count, block_len, head_count, head_width)

    query_rows = split_heads(queries)
    key_rows = split_heads(keys)
    value_rows = split_heads(values)
    grad_rows = split_heads(out_grad)
    carry_all, local_state, state_pull = jax.vmap(block_summary)(
        query_rows, key_rows, value_rows, grad_rows, tables
    )
    identity = (jnp.ones_like(carry_all), jnp.zeros_like(local_state))
    states_in = carried_in((carry_all, local_state), "ctx", compose, identity, False)[1]
    state_grads = carried_in((carry_all, state_pull), "ctx", compose, identity, True)[1]
    attention, query_grad, key_grad, value_grad = jax.vmap(block_outputs)(
        query_rows, key_rows, value_rows, grad_rows, tables, states_in, state_grads
    )
    attention = attention.reshape(seq_count, block_len, features)
    normed = (
        attention
        * lax.rsqrt(jnp.mean(attention * attention, axis=-1, keepdims=True) + norm_eps)
        * norm_gain
    ).astype(jnp.bfloat16)
    data_count = lax.axis_size("dp")
    ctx_count = lax.axis_size("ctx")
    grad_scale = 1.0 / math.sqrt(seq_count * block_len * data_count * ctx_count)
    normed_rows = normed.reshape(seq_count * block_len, features)
    layer_rows = layer_grad.reshape(seq_count * block_len, layer_grad.shape[2])
    product = lax.dot_general(
        normed_rows, layer_rows, (((0,), (0,)), ((), ())), preferred_element_type=jnp.float32
    )
    proj_grad = lax.psum_scatter(
        product * grad_scale, ("dp", "ctx"), scatter_dimension=0, tiled=True
    )
    shape_out = (seq_count, block_len, features)
    return (
        query_grad.reshape(shape_out).astype(jnp.bfloat16),
        key_grad.reshape(shape_out).astype(jnp.bfloat16),
        value_grad.reshape(shape_out).astype(jnp.bfloat16),
        proj_grad,
    )


def solution(mesh):
    return jax.shard_map(
        on_device,
        mesh=mesh,
        in_specs=(
            P("dp", "ctx", None),
            P("dp", "ctx", None),
            P("dp", "ctx", None),
            P("dp", "ctx", None),
            P("dp", "ctx", None),
            P(),
            P(),
            P("dp", None),
        ),
        out_specs=(
            P("dp", "ctx", None),
            P("dp", "ctx", None),
            P("dp", "ctx", None),
            P(("dp", "ctx"), None),
        ),
        check_vma=False,
    )
```

profile of v0, /device:TPU:1, one launch (start us, length us, event | category | flops | bytes accessed | tf_op | source)
XLA Modules:
  0.0 707.5 jit_solution(11935270671122139635)
XLA Ops:
  11.7 1.3 broadcast_compare_fusion.1
  14.3 1.3 dynamic-slice
  17.1 1.5 fusion.20
  19.9 1.5 fusion.17
  21.5 77.1 %all-reduce = f32[256]{0:T(256)S(1)} all-reduce(f32[256]{0:T(256)S(1)} %get-tuple-element.349), channel_id=2, replica_groups=mesh['dp'=16,'ctx'=32] {'ctx'}, use_global_device_ids=true, to_apply=%add | all-reduce | flops 256 | bytes 2048
  99.4 122.0 %all-gather.6.cloned.1.call-done = f32[256,128,128]{2,1,0:T(8,128)} async-done(((f32[8,128,128]{2,1,0:T(8,128)}), f32[256,128,128]{2,1,0:T(8,128)}) %all-gather.6.cloned.1.call-update) | async-done | bytes 16777232 | tf_op jit(solution)/shard_map/all_gather | solution.py:14
  221.3 38.8 %while.30 = (s32[]{:T(128)}, f32[1,8,128,128]{3,2,1,0:T(8,128)S(1)}, s32[]{:T(128)}, f32[32,1,8]{2,1,0:T(1,128)S(1)}, f32[32,1,8,128,128]{4,3,2,1,0:T(8,128)}, /*index=5*/s32[]{:T(128)}, s32[]{:T(128)}) while((s32[]{:T(128)}, f32[1,8,128,128]{3,2,1,0:T(8,128)S(1)}, s32[]{:T(128)}, f32[32,1,8]{2,1,0:T(1,128)S(1)}, ...), condition=%wide.region_4.5_spmd.clone, body=%wide.region_3.4_spmd.clone.sunk | while | flops 524292 | bytes 1573065 | solution.py:27
  243.2 1.2 fusion.54
  244.4 1.2 fusion.54
  245.6 1.2 fusion.54
  251.7 1.2 fusion.54
  252.9 1.2 fusion.54
  254.1 1.2 fusion.54
  261.7 2.2 convolution_multiply_fusion
  264.0 151.3 %all-gather.8.cloned.1.call-done = f32[256,128,128]{2,1,0:T(8,128)} async-done(((f32[8,128,128]{2,1,0:T(8,128)}), f32[256,128,128]{2,1,0:T(8,128)}) %all-gather.8.cloned.1.call-update) | async-done | bytes 16777232 | tf_op jit(solution)/shard_map/all_gather | solution.py:14
  415.3 39.2 %while.31 = (s32[]{:T(128)}, f32[1,8,128,128]{3,2,1,0:T(8,128)S(1)}, s32[]{:T(128)}, f32[32,1,8]{2,1,0:T(1,128)S(1)}, f32[32,1,8,128,128]{4,3,2,1,0:T(8,128)}, /*index=5*/s32[]{:T(128)}, s32[]{:T(128)}, s32[]{:T(128)}, s32[]{:T(128)}) while((s32[]{:T(128)}, f32[1,8,128,128]{3,2,1,0:T(8,128)S(1)}, s32[]{:T(128)}, ...), condition=%wide.region_6.7_spmd.clone, body=%wide.region_5.6_spmd.clone.sunk | while | flops 524296 | bytes 1573127 | solution.py:27
  430.0 1.2 fusion.55
  433.6 1.2 fusion.55
  434.9 1.2 fusion.55
  442.2 1.2 fusion.55
  445.9 1.2 fusion.55
  447.2 1.2 fusion.55
  460.0 239.6 %all-reduce.4.cloned.1.call-done = f32[1024,768]{1,0:T(8,128)} async-done(((f32[1024,768]{1,0:T(8,128)}), f32[1024,768]{1,0:T(8,128)}) %all-reduce.4.cloned.1.call-update) | async-done | bytes 3145744
  699.6 1.3 constant_dynamic-slice_fusion
  (161 shorter events, 76.0 us)
Async XLA Ops:
  7.2 254.6 %copy-start = (bf16[1,128,768]{2,1,0:T(8,128)(2,1)S(1)}, bf16[1,128,768]{2,1,0:T(8,128)(2,1)}, u32[]{:S(2)}) copy-start(bf16[1,128,768]{2,1,0:T(8,128)(2,1)} %param.16) | copy-start | bytes 589828
  7.2 12.6 %copy-start.1 = (bf16[1,128,1024]{2,1,0:T(8,128)(2,1)S(1)}, bf16[1,128,1024]{2,1,0:T(8,128)(2,1)}, u32[]{:S(2)}) copy-start(bf16[1,128,1024]{2,1,0:T(8,128)(2,1)} %param.15) | copy-start | bytes 786436
  7.2 214.2 %all-gather.6.cloned.1.call-start = ((), (), s32[]{:S(2)}) async-start(), calls=%async_computation | async-start | bytes 17301504 | tf_op jit(solution)/shard_map/all_gather | solution.py:14
  18.6 396.7 %all-gather.8.cloned.1.call-start = ((), (), s32[]{:S(2)}) async-start(), calls=%async_computation.1 | async-start | bytes 17301504 | tf_op jit(solution)/shard_map/all_gather | solution.py:14
  21.4 678.2 %all-reduce.4.cloned.1.call-start = ((), (), s32[]{:S(2)}) async-start(), calls=%async_computation.2 | async-start | bytes 6291456
  260.2 1.3 copy-start.2
Sparse Core Ops, SparseCore 0:
  18.7 202.6 all-gather.5
  223.4 191.7 all-gather.7
  420.3 279.3 all-reduce.3
where the time goes:
time: 711 us; the launch traced here: 707 us
  waiting for transfers between devices  513 us (72%)
  other arithmetic  79.3 us (11%)
  blocking collectives  77.1 us (11%)
  between operations  15.9 us (2%)
  matrix products  9.96 us (1%)
  local copies, waits for them, and re-layouts  9.82 us (1%)
    all_gather x2, waiting for transfers between devices, carried_in(): everything = jax.tree.map(lambda part: lax.all_gather(part, axis), value)  273 us
    unnamed x4, waiting for transfers between devices  240 us
    unnamed x1, blocking collectives  77.1 us
    select_n x64, other arithmetic, lap(): return jax.tree.map(lambda a, b: jnp.where(reached, a, b), new, before)  75.3 us
  transfers between devices with their start and end apart: 3, of which 3 were waited for; matrix products, arithmetic and copies ran while one was open for 13% of the time, Pallas kernels for 0%

commit v1 on v0

v1 whole, which is shorter than its diff:
```python
import functools
import math

import jax
import jax.numpy as jnp
from jax import lax
from jax.experimental import pallas as pl
from jax.experimental.pallas import tpu as pltpu
from jax.sharding import PartitionSpec as P

norm_eps = 1e-06
HEADS, WIDTH, ROWS = 8, 128, 128
NX, NZ, NY, NZL = 4, 8, 8, 4
MESH = pl.DeviceIdType.MESH
f32, bf16 = jnp.float32, jnp.bfloat16
VMEM_SPEC = pl.BlockSpec(memory_space=pltpu.VMEM)
SMEM_SPEC = pl.BlockSpec(memory_space=pltpu.SMEM)


def split(value):
    high = value.astype(bf16)
    return high, (value - high.astype(f32)).astype(bf16)


def matmul(a, b, dims):
    return lax.dot_general(a, b, (dims, ((), ())), preferred_element_type=f32)


NN, NT, TN = ((1,), (0,)), ((1,), (1,)), ((0,), (0,))


def doc_bounds(len_ref):
    first = len_ref[0, 0]
    second = first + len_ref[0, 1]
    return first, second, second + len_ref[0, 2]


def doc_of(positions, bounds):
    return sum((positions >= bound).astype(jnp.int32) for bound in bounds)


def doc_of_scalar(position, bounds):
    return sum(jnp.where(position >= bound, 1, 0) for bound in bounds)


def edge_tables(base, bounds):
    offsets = lax.broadcasted_iota(jnp.int32, (ROWS, WIDTH), 0)
    docs = doc_of(base + offsets, bounds)
    entering = docs == doc_of_scalar(base - 1, bounds)
    leaving = docs == doc_of_scalar(base + ROWS - 1, bounds)
    return offsets.astype(f32), entering, leaving


def summary_kernel(q_ref, k_ref, v_ref, g_ref, rate_ref, len_ref, state_ref, pull_ref, carry_ref):
    ctx = lax.axis_index("ctx")
    bounds = doc_bounds(len_ref)
    offsets, entering, leaving = edge_tables(ctx * ROWS, bounds)
    for h in range(HEADS):
        cols = pl.ds(h * WIDTH, WIDTH)
        rate = rate_ref[h]
        entry = jnp.where(entering, jnp.exp(-rate * offsets), 0.0)
        leave = jnp.where(leaving, jnp.exp(-rate * (ROWS - offsets)), 0.0)
        high, low = split(k_ref[:, cols].astype(f32) * leave)
        v = v_ref[:, cols]
        state_ref[h] = matmul(high, v, TN) + matmul(low, v, TN)
        high, low = split(q_ref[:, cols].astype(f32) * entry)
        g = g_ref[:, cols]
        pull_ref[h] = matmul(high, g, TN) + matmul(low, g, TN)
    group, own = ctx // NY, lax.rem(ctx, NY)
    rate = rate_ref[own]

    def carry(first, blocks):
        start = first * ROWS
        whole = doc_of_scalar(start - 1, bounds) == doc_of_scalar(start + blocks * ROWS - 1, bounds)
        decay = jnp.exp(jnp.full((1, WIDTH), -rate * float(blocks * ROWS), f32))
        return jnp.where(whole, decay, 0.0)

    for j in range(NY):
        carry_ref[pl.ds(j, 1), :] = carry(group * NY + j, 1)
    carry_ref[pl.ds(8, 1), :] = carry((group - 1) * NY, NY)
    carry_ref[pl.ds(9, 1), :] = carry((group + 1) * NY, NY)


def scan_kernel(
    state_ref, pull_ref, carry_ref, in_ref, grad_ref,
    state_buf, pull_buf, in_buf, grad_buf, total_buf, group_buf,
    out_send, out_recv, back_send, back_recv, group_send, group_recv,
):
    dp, ctx = lax.axis_index("dp"), lax.axis_index("ctx")
    z, y = ctx // NY, lax.rem(ctx, NY)
    barrier = pltpu.get_barrier_semaphore()

    def at_y(k):
        return (dp, z * NY + lax.rem(y + k, NY))

    for k in range(1, NY):
        pl.semaphore_signal(barrier, inc=1, device_id=at_y(k), device_id_type=MESH)
    for k in range(1, NZL):
        there = (dp, lax.rem(z + k, NZL) * NY + y)
        pl.semaphore_signal(barrier, inc=1, device_id=there, device_id_type=MESH)
    pl.semaphore_wait(barrier, NY - 1 + NZL - 1)

    def send(src, dst, send_sem, recv_sem, device):
        return pltpu.make_async_remote_copy(
            src_ref=src, dst_ref=dst, send_sem=send_sem, recv_sem=recv_sem,
            device_id=device, device_id_type=MESH,
        )

    out_copies = []
    for d, (src, buf) in enumerate(((state_ref, state_buf), (pull_ref, pull_buf))):
        for k in range(1, NY):
            copy = send(
                src.at[lax.rem(y + k, NY)], buf.at[k], out_send.at[d, k], out_recv.at[d, k], at_y(k)
            )
            copy.start()
            out_copies.append(copy)

    def carry(j):
        return carry_ref[pl.ds(j, 1), :]

    def slot(j):
        return lax.rem(y - j + NY, NY)

    orders = (tuple(range(NY)), tuple(reversed(range(NY))))
    steps = (1, -1)

    def group_copy(d, far):
        there = (dp, (z + steps[d] * far) * NY + y)
        return send(
            total_buf.at[d], group_buf.at[d, far - 1],
            group_send.at[d, far - 1], group_recv.at[d, far - 1], there,
        )

    for d, (src, buf) in enumerate(((state_ref, state_buf), (pull_ref, pull_buf))):
        buf[0] = src[y]
        for copy in out_copies[d * (NY - 1):(d + 1) * (NY - 1)]:
            copy.wait_recv()
        total = jnp.zeros((WIDTH, WIDTH), f32)
        for j in orders[d]:
            total = carry(j) * total + buf[slot(j)]
        total_buf[d] = total
        for far in (1, 2):
            has_target = z + far < NZL if d == 0 else z - far >= 0

            @pl.when(has_target)
            def _():
                group_copy(d, far).start()

    back_copies = []
    for d, (buf, back, result) in enumerate(((state_buf, in_buf, in_ref), (pull_buf, grad_buf, grad_ref))):
        for far in (1, 2):
            has_source = z - far >= 0 if d == 0 else z + far < NZL

            @pl.when(has_source)
            def _():
                group_copy(d, far).wait_recv()

            @pl.when(jnp.logical_not(has_source))
            def _():
                group_buf[d, far - 1] = jnp.zeros((WIDTH, WIDTH), f32)

        now = group_buf[d, 0] + carry(8 + d) * group_buf[d, 1]
        for j in orders[d]:
            back[j] = now
            if j != orders[d][-1]:
                now = carry(j) * now + buf[slot(j)]
        for k in range(1, NY):
            copy = send(
                back.at[lax.rem(y + k, NY)], result.at[y],
                back_send.at[d, k], back_recv.at[d, k], at_y(k),
            )
            copy.start()
            back_copies.append((d, k, copy))
        result[y] = back[y]

    for d, k, copy in back_copies:
        result = (in_ref, grad_ref)[d]
        arrived = send(
            in_buf.at[0], result.at[lax.rem(y - k + NY, NY)],
            back_send.at[d, k], back_recv.at[d, k], at_y(k),
        )
        arrived.wait_recv()
    for d in range(2):
        for far in (1, 2):
            has_target = z + far < NZL if d == 0 else z - far >= 0

            @pl.when(has_target)
            def _():
                group_copy(d, far).wait_send()
    for copy in out_copies:
        copy.wait_send()
    for _, _, copy in back_copies:
        copy.wait_send()


def outputs_kernel(
    q_ref, k_ref, v_ref, g_ref, layer_ref, gain_ref, rate_ref, len_ref, in_ref, grad_ref,
    dq_ref, dk_ref, dv_ref, product_ref, attention_buf, normed_buf,
):
    base = lax.axis_index("ctx") * ROWS
    bounds = doc_bounds(len_ref)
    offsets, entering, leaving = edge_tables(base, bounds)
    rows = lax.broadcasted_iota(jnp.int32, (ROWS, ROWS), 0)
    columns = lax.broadcasted_iota(jnp.int32, (ROWS, ROWS), 1)
    same = (doc_of(base + rows, bounds) == doc_of(base + columns, bounds)) & (rows >= columns)
    distance = jnp.maximum(rows - columns, 0).astype(f32)
    for h in range(HEADS):
        cols = pl.ds(h * WIDTH, WIDTH)
        rate = rate_ref[h]
        q, k, v, g = q_ref[:, cols], k_ref[:, cols], v_ref[:, cols], g_ref[:, cols]
        mask = jnp.where(same, jnp.exp(-rate * distance), 0.0)
        entry = jnp.where(entering, jnp.exp(-rate * offsets), 0.0)
        leave = jnp.where(leaving, jnp.exp(-rate * (ROWS - offsets)), 0.0)
        s_high, s_low = split(matmul(q, k, NT) * mask)
        d_high, d_low = split(matmul(g, v, NT) * mask)
        in_high, in_low = split(in_ref[h])
        grad_high, grad_low = split(grad_ref[h])
        attention = matmul(s_high, v, NN) + matmul(s_low, v, NN)
        attention += entry * (matmul(q, in_high, NN) + matmul(q, in_low, NN))
        attention_buf[:, cols] = attention
        dq = matmul(d_high, k, NN) + matmul(d_low, k, NN)
        dq += entry * (matmul(g, in_high, NT) + matmul(g, in_low, NT))
        dq_ref[:, cols] = dq.astype(bf16)
        dk = matmul(d_high, q, TN) + matmul(d_low, q, TN)
        dk += leave * (matmul(v, grad_high, NT) + matmul(v, grad_low, NT))
        dk_ref[:, cols] = dk.astype(bf16)
        dv = matmul(s_high, g, TN) + matmul(s_low, g, TN)
        dv += leave * (matmul(k, grad_high, NN) + matmul(k, grad_low, NN))
        dv_ref[:, cols] = dv.astype(bf16)
    attention = attention_buf[...]
    mean = jnp.mean(attention * attention, axis=-1, keepdims=True)
    normed_buf[...] = (attention * lax.rsqrt(mean + norm_eps) * gain_ref[...]).astype(bf16)
    for h in range(HEADS):
        cols = pl.ds(h * WIDTH, WIDTH)
        product_ref[cols, :] = matmul(normed_buf[:, cols], layer_ref[...], TN)


def reduce_kernel(
    scale, p_ref, out_ref, core_buf, a_buf, x_buf, b_buf, z_buf, c_buf, y_buf,
    core_send, core_recv, x_send, x_recv, z_send, z_recv, y_send, y_recv,
):
    dp, ctx = lax.axis_index("dp"), lax.axis_index("ctx")
    x, z_high, core = dp // 4, lax.rem(dp // 2, 2), lax.rem(dp, 2)
    z, y = z_high * 4 + ctx // NY, lax.rem(ctx, NY)
    twin = (dp + 1 - 2 * core, ctx)

    def at_x(k):
        return (lax.rem(x + k, NX) * 4 + lax.rem(dp, 4), ctx)

    def at_z(k):
        there = lax.rem(z + k, NZ)
        return (x * 4 + there // 4 * 2 + core, lax.rem(there, 4) * NY + y)

    def at_y(k):
        return (dp, ctx - y + lax.rem(y + k, NY))

    barrier = pltpu.get_barrier_semaphore()
    pl.semaphore_signal(barrier, inc=1, device_id=twin, device_id_type=MESH)
    for at, count in ((at_x, NX), (at_z, NZ), (at_y, NY)):
        for k in range(1, count):
            pl.semaphore_signal(barrier, inc=1, device_id=at(k), device_id_type=MESH)
    pl.semaphore_wait(barrier, NX + NZ + NY - 2)

    def send(src, dst, sems, k, device):
        copy = pltpu.make_async_remote_copy(
            src_ref=src, dst_ref=dst, send_sem=sems[0].at[k], recv_sem=sems[1].at[k],
            device_id=device, device_id_type=MESH,
        )
        copy.start()
        return copy

    order = tuple(range(1, NX)) + (0,)
    core_copies, copies = [], []
    for k in order:
        there = lax.rem(x + k, NX)
        core_copies.append(
            send(p_ref.at[there, :, 1 - core], core_buf.at[k], (core_send, core_recv), k, twin)
        )
    x_copies = []
    for k, copy in zip(order, core_copies):
        copy.wait_recv()
        a_buf[k] = p_ref[lax.rem(x + k, NX), :, core] + core_buf[k]
        if k:
            x_copies.append(send(a_buf.at[k], x_buf.at[k], (x_send, x_recv), k, at_x(k)))
    total = a_buf[0]
    for k, copy in enumerate(x_copies, 1):
        copy.wait_recv()
        total = total + x_buf[k]
    b_buf[...] = total.reshape(b_buf.shape)
    z_copies = [
        send(b_buf.at[lax.rem(z + k, NZ)], z_buf.at[k], (z_send, z_recv), k, at_z(k))
        for k in range(1, NZ)
    ]
    total = b_buf[z]
    for k, copy in enumerate(z_copies, 1):
        copy.wait_recv()
        total = total + z_buf[k]
    for j in range(NY):
        c_buf[j] = total[2 * j:2 * j + 2, :]
    y_copies = [
        send(c_buf.at[lax.rem(y + k, NY)], y_buf.at[k], (y_send, y_recv), k, at_y(k))
        for k in range(1, NY)
    ]
    total = c_buf[y]
    for k, copy in enumerate(y_copies, 1):
        copy.wait_recv()
        total = total + y_buf[k]
    out_ref[...] = total * scale
    for copy in core_copies + x_copies + z_copies + y_copies:
        copy.wait_send()


def on_device(queries, keys, values, out_grad, layer_grad, norm_gain, decay_rates, doc_lengths):
    rows, features, bucket = ROWS, HEADS * WIDTH, layer_grad.shape[2]
    scale = 1.0 / math.sqrt(rows * lax.axis_size("dp") * lax.axis_size("ctx"))
    q, k, v, g = (a.reshape(rows, features) for a in (queries, keys, values, out_grad))
    layer = layer_grad.reshape(rows, bucket)
    states = jax.ShapeDtypeStruct((HEADS, WIDTH, WIDTH), f32)
    heads_buf = pltpu.VMEM((HEADS, WIDTH, WIDTH), f32)
    state, pull, carry = pl.pallas_call(
        summary_kernel,
        out_shape=(states, states, jax.ShapeDtypeStruct((16, WIDTH), f32)),
        in_specs=[VMEM_SPEC] * 4 + [SMEM_SPEC] * 2,
        out_specs=(VMEM_SPEC,) * 3,
        name="summary",
    )(q, k, v, g, decay_rates, doc_lengths)
    state_in, state_grad = pl.pallas_call(
        scan_kernel,
        out_shape=(states, states),
        in_specs=[VMEM_SPEC] * 3,
        out_specs=(VMEM_SPEC,) * 2,
        scratch_shapes=[heads_buf] * 4
        + [pltpu.VMEM((2, WIDTH, WIDTH), f32), pltpu.VMEM((2, 2, WIDTH, WIDTH), f32)]
        + [pltpu.SemaphoreType.DMA((2, NY))] * 4
        + [pltpu.SemaphoreType.DMA((2, 2))] * 2,
        compiler_params=pltpu.CompilerParams(collective_id=0, has_side_effects=True),
        name="scan",
    )(state, pull, carry)
    grad_shape = jax.ShapeDtypeStruct((rows, features), bf16)
    query_grad, key_grad, value_grad, product = pl.pallas_call(
        outputs_kernel,
        out_shape=(grad_shape,) * 3 + (jax.ShapeDtypeStruct((features, bucket), f32),),
        in_specs=[VMEM_SPEC] * 6 + [SMEM_SPEC] * 2 + [VMEM_SPEC] * 2,
        out_specs=(VMEM_SPEC,) * 4,
        scratch_shapes=[pltpu.VMEM((rows, features), f32), pltpu.VMEM((rows, features), bf16)],
        name="outputs",
    )(q, k, v, g, layer, norm_gain.reshape(1, features), decay_rates, doc_lengths, state_in, state_grad)
    proj_grad = pl.pallas_call(
        functools.partial(reduce_kernel, scale),
        out_shape=jax.ShapeDtypeStruct((2, bucket), f32),
        in_specs=[VMEM_SPEC],
        out_specs=VMEM_SPEC,
        scratch_shapes=[
            pltpu.VMEM((NX, 2, 64, bucket), f32),
            pltpu.VMEM((NX, 2, 64, bucket), f32),
            pltpu.VMEM((NX, 2, 64, bucket), f32),
            pltpu.VMEM((NZ, 16, bucket), f32),
            pltpu.VMEM((NZ, 16, bucket), f32),
            pltpu.VMEM((NY, 2, bucket), f32),
            pltpu.VMEM((NY, 2, bucket), f32),
        ]
        + [pltpu.SemaphoreType.DMA((NX,))] * 4
        + [pltpu.SemaphoreType.DMA((NZ,))] * 2
        + [pltpu.SemaphoreType.DMA((NY,))] * 2,
        compiler_params=pltpu.CompilerParams(collective_id=1, has_side_effects=True),
        name="reduce",
    )(product.reshape(NX, 2, 2, 64, bucket))
    shape_out = (1, rows, features)
    return (
        query_grad.reshape(shape_out),
        key_grad.reshape(shape_out),
        value_grad.reshape(shape_out),
        proj_grad,
    )


def solution(mesh):
    block = P("dp", "ctx", None)
    return jax.shard_map(
        on_device,
        mesh=mesh,
        in_specs=(block,) * 5 + (P(), P(), P("dp", None)),
        out_specs=(block,) * 3 + (P(("dp", "ctx"), None),),
        check_vma=False,
    )
```

time: 711 us -> 122 us (0.17)
  waiting for transfers between devices: 513 us -> 0 us
  Pallas kernels: 0 us -> 119 us
  other arithmetic: 79.3 us -> 0 us
  blocking collectives: 77.1 us -> 0 us
  between operations: 15.9 us -> 0.65 us
  matrix products: 9.96 us -> 0 us
  local copies, waits for them, and re-layouts: 9.82 us -> 1.29 us
    all_gather x2 -> x0, waiting for transfers between devices: 273 us -> none  [carried_in(): everything = jax.tree.map(lambda part: lax.all_gather(part, axis), value)]
    unnamed x4 -> x0, waiting for transfers between devices: 240 us -> none
    pallas_call x0 -> x4, Pallas kernels: none -> 119 us  [the longest x1 58.9 us: on_device(): pl.pallas_call(scan_kernel, out_shape=(states, states), in_specs=[VMEM_SP...]
    unnamed x1 -> x0, blocking collectives: 77.1 us -> none
    select_n x64 -> x0, other arithmetic: 75.3 us -> none  [lap(): return jax.tree.map(lambda a, b: jnp.where(reached, a, b), new, before)]
    dot_general x13 -> x0, matrix products: 9.96 us -> none  [the longest x1 2.25 us: on_device(): lax.dot_general(normed_rows, layer_rows, (((0,), (0,)), ((), ())), prefer...]
  transfers between devices with their start and end apart: 3 -> 0, of which waited for: 3 -> 0; matrix products, arithmetic and copies ran while one was open for 13% -> 0% of each run, Pallas kernels for 0% -> 0%
where the time goes in v1:
time: 122 us; the launch traced here: 121 us
  Pallas kernels  119 us (98%)
  local copies, waits for them, and re-layouts  1.29 us (1%)
    pallas_call x1, Pallas kernels, on_device(): pl.pallas_call(scan_kernel, out_shape=(states, states), in_specs=[VMEM_SP...  58.9 us
    pallas_call x1, Pallas kernels, on_device(): pl.pallas_call(functools.partial(reduce_kernel, scale), out_shape=jax.Sha...  51.1 us
    pallas_call x1, Pallas kernels, on_device(): pl.pallas_call(outputs_kernel, out_shape=(grad_shape,) * 3 + (jax.ShapeDt...  6.6 us
    pallas_call x1, Pallas kernels, on_device(): pl.pallas_call(summary_kernel, out_shape=(states, states, jax.ShapeDtypeS...  2.79 us

profile of v1, /device:TPU:1, one launch (start us, length us, event | category | flops | bytes accessed | tf_op | source)
XLA Modules:
  0.0 121.3 jit_solution(9990408025752671018)
XLA Ops:
  0.6 2.8 %summary.1 = (f32[8,128,128]{2,1,0:T(8,128)}, f32[8,128,128]{2,1,0:T(8,128)}, f32[16,128]{1,0:T(8,128)}) custom-call(bf16[128,1024]{1,0:T(8,128)(2,1)} %bitcast.11, bf16[128,1024]{1,0:T(8,128)(2,1)} %bitcast.13, bf16[128,1024]{1,0:T(8,128)(2,1)} %bitcast.15, bf16[128,1024]{1,0:T(8,128)(2,1)} %bitcast.17, f32[8]{0:T(128)} %rate_ref.3, s32[1,4]{1,0:T(1,128)} %len_ref.3), custom_call_target="tpu_custom_call" | custom-call | tf_op jit(solution)/shard_map/summary/pallas_call | solution.py:320
  3.4 58.9 %scan.1 = (f32[8,128,128]{2,1,0:T(8,128)}, f32[8,128,128]{2,1,0:T(8,128)}) custom-call(f32[8,128,128]{2,1,0:T(8,128)} %get-tuple-element.13.state_ref, f32[8,128,128]{2,1,0:T(8,128)} %get-tuple-element.14.pull_ref, f32[16,128]{1,0:T(8,128)} %get-tuple-element.15.carry_ref), custom_call_target="tpu_custom_call" | custom-call | tf_op jit(solution)/shard_map/scan/pallas_call | solution.py:327
  62.3 6.6 %outputs.1 = (bf16[128,1024]{1,0:T(8,128)(2,1)}, bf16[128,1024]{1,0:T(8,128)(2,1)}, bf16[128,1024]{1,0:T(8,128)(2,1)}, f32[1024,768]{1,0:T(8,128)}) custom-call(bf16[128,1024]{1,0:T(8,128)(2,1)} %bitcast.12, bf16[128,1024]{1,0:T(8,128)(2,1)} %bitcast.14, bf16[128,1024]{1,0:T(8,128)(2,1)} %bitcast.16, bf16[128,1024]{1,0:T(8,128)(2,1)} %bitcast.18, ...), custom_call_target="tpu_custom_call" | custom-call | tf_op jit(solution)/shard_map/outputs/pallas_call | solution.py:340
  68.9 51.1 %reduce.1 = f32[2,768]{1,0:T(2,128)} custom-call(f32[4,2,2,64,768]{4,3,2,1,0:T(8,128)} %bitcast.10), custom_call_target="tpu_custom_call" | custom-call | tf_op jit(solution)/shard_map/reduce/pallas_call | solution.py:348
  120.0 1.3 %copy.13 = f32[2,768]{1,0:T(2,128)} copy(f32[2,768]{1,0:T(2,128)} %reduce.1) | data formatting | bytes 12288

commit v2 on v1

v2 whole, which is shorter than its diff:
```python
import functools
import math

import jax
import jax.numpy as jnp
from jax import lax
from jax.experimental import pallas as pl
from jax.experimental.pallas import tpu as pltpu
from jax.sharding import PartitionSpec as P

norm_eps = 1e-06
HEADS, WIDTH, ROWS = 8, 128, 128
NX, NZ, NY, NZL = 4, 8, 8, 4
XCOLS = 512
MESH = pl.DeviceIdType.MESH
f32, bf16 = jnp.float32, jnp.bfloat16
VMEM_SPEC = pl.BlockSpec(memory_space=pltpu.VMEM)
SMEM_SPEC = pl.BlockSpec(memory_space=pltpu.SMEM)


def split(value):
    high = value.astype(bf16)
    return high, (value - high.astype(f32)).astype(bf16)


def matmul(a, b, dims):
    return lax.dot_general(a, b, (dims, ((), ())), preferred_element_type=f32)


NN, NT, TN = ((1,), (0,)), ((1,), (1,)), ((0,), (0,))


def doc_bounds(len_ref):
    first = len_ref[0, 0]
    second = first + len_ref[0, 1]
    return first, second, second + len_ref[0, 2]


def doc_of(positions, bounds):
    return sum((positions >= bound).astype(jnp.int32) for bound in bounds)


def doc_of_scalar(position, bounds):
    return sum(jnp.where(position >= bound, 1, 0) for bound in bounds)


def edge_tables(base, bounds):
    offsets = lax.broadcasted_iota(jnp.int32, (ROWS, WIDTH), 0)
    docs = doc_of(base + offsets, bounds)
    entering = docs == doc_of_scalar(base - 1, bounds)
    leaving = docs == doc_of_scalar(base + ROWS - 1, bounds)
    return offsets.astype(f32), entering, leaving


def summary_kernel(q_ref, k_ref, v_ref, g_ref, rate_ref, len_ref, state_ref, pull_ref, carry_ref):
    ctx = lax.axis_index("ctx")
    bounds = doc_bounds(len_ref)
    offsets, entering, leaving = edge_tables(ctx * ROWS, bounds)
    for h in range(HEADS):
        cols = pl.ds(h * WIDTH, WIDTH)
        rate = rate_ref[h]
        entry = jnp.where(entering, jnp.exp(-rate * offsets), 0.0)
        leave = jnp.where(leaving, jnp.exp(-rate * (ROWS - offsets)), 0.0)
        high, low = split(k_ref[:, cols].astype(f32) * leave)
        v = v_ref[:, cols]
        state_ref[h] = matmul(high, v, TN) + matmul(low, v, TN)
        high, low = split(q_ref[:, cols].astype(f32) * entry)
        g = g_ref[:, cols]
        pull_ref[h] = matmul(high, g, TN) + matmul(low, g, TN)
    group, own = ctx // NY, lax.rem(ctx, NY)
    rate = rate_ref[own]

    def carry(first, blocks):
        start = first * ROWS
        whole = doc_of_scalar(start - 1, bounds) == doc_of_scalar(start + blocks * ROWS - 1, bounds)
        decay = jnp.exp(jnp.full((1, WIDTH), -rate * float(blocks * ROWS), f32))
        return jnp.where(whole, decay, 0.0)

    for j in range(NY):
        carry_ref[pl.ds(j, 1), :] = carry(group * NY + j, 1)
    carry_ref[pl.ds(8, 1), :] = carry((group - 1) * NY, NY)
    carry_ref[pl.ds(9, 1), :] = carry((group + 1) * NY, NY)


def place():
    dp, ctx = lax.axis_index("dp"), lax.axis_index("ctx")
    return dp, ctx, ctx // NY, lax.rem(ctx, NY)


def send(src, dst, sems, at, device):
    return pltpu.make_async_remote_copy(
        src_ref=src, dst_ref=dst, send_sem=sems[0].at[at], recv_sem=sems[1].at[at],
        device_id=device, device_id_type=MESH,
    )


def started(copies):
    for copy in copies:
        copy.start()
    return copies


class Scan:
    def __init__(self, step, src, carry, result, bufs, out_sems, back_sems, group_sems):
        self.step, self.src, self.carry_ref, self.result = step, src, carry, result
        self.buf, self.back, self.total, self.group = bufs
        self.out_sems, self.back_sems, self.group_sems = out_sems, back_sems, group_sems
        self.dp, _, self.z, self.y = place()
        self.order = range(NY) if step > 0 else range(NY - 1, -1, -1)

    def at_y(self, k):
        return (self.dp, self.z * NY + lax.rem(self.y + k, NY))

    def carry(self, j):
        return self.carry_ref[pl.ds(j, 1), :]

    def block(self, j):
        return self.buf[lax.rem(self.y - j + NY, NY)]

    def scatter(self):
        self.out_copies = started([
            send(self.src.at[lax.rem(self.y + k, NY)], self.buf.at[k], self.out_sems, k, self.at_y(k))
            for k in range(1, NY)
        ])
        self.buf[0] = self.src[self.y]

    def group_copy(self, far):
        there = (self.dp, (self.z + self.step * far) * NY + self.y)
        return send(self.total, self.group.at[far - 1], self.group_sems, far - 1, there)

    def has(self, far):
        other = self.z + far
        return (other >= 0) & (other < NZL)

    def totals(self):
        for copy in self.out_copies:
            copy.wait_recv()
        total = jnp.zeros((WIDTH, WIDTH), f32)
        for j in self.order:
            total = self.carry(j) * total + self.block(j)
        self.total[...] = total
        for far in (1, 2):
            pl.when(self.has(self.step * far))(lambda far=far: self.group_copy(far).start())

    def give_back(self):
        for far in (1, 2):
            source = self.has(-self.step * far)
            pl.when(source)(lambda far=far: self.group_copy(far).wait_recv())

            @pl.when(jnp.logical_not(source))
            def _():
                self.group[far - 1] = jnp.zeros((WIDTH, WIDTH), f32)

        now = self.group[0] + self.carry(8 if self.step > 0 else 9) * self.group[1]
        for j in self.order:
            self.back[j] = now
            now = self.carry(j) * now + self.block(j)
        self.back_copies = started([
            send(self.back.at[lax.rem(self.y + k, NY)], self.result.at[self.y], self.back_sems, k, self.at_y(k))
            for k in range(1, NY)
        ])
        self.result[self.y] = self.back[self.y]

    def finish(self):
        for k in range(1, NY):
            send(
                self.back.at[0], self.result.at[lax.rem(self.y - k + NY, NY)],
                self.back_sems, k, self.at_y(k),
            ).wait_recv()
        for far in (1, 2):
            pl.when(self.has(self.step * far))(lambda far=far: self.group_copy(far).wait_send())
        for copy in self.out_copies + self.back_copies:
            copy.wait_send()


HEADS_BUF = pltpu.VMEM((HEADS, WIDTH, WIDTH), f32)
SCAN_BUFS = [HEADS_BUF, HEADS_BUF, pltpu.VMEM((WIDTH, WIDTH), f32), pltpu.VMEM((2, WIDTH, WIDTH), f32)]
SCAN_SEMS = [pltpu.SemaphoreType.DMA((NY,))] * 4 + [pltpu.SemaphoreType.DMA((2,))] * 2


def greet(devices):
    barrier = pltpu.get_barrier_semaphore()
    for device in devices:
        pl.semaphore_signal(barrier, inc=1, device_id=device, device_id_type=MESH)
    pl.semaphore_wait(barrier, len(devices))


def scan_kernel(state_ref, carry_ref, in_ref, *scratch):
    dp, ctx, z, y = place()
    scan = Scan(1, state_ref, carry_ref, in_ref, scratch[:4], scratch[4:6], scratch[6:8], scratch[8:10])
    greet(
        [scan.at_y(k) for k in range(1, NY)]
        + [(dp, lax.rem(z + k, NZL) * NY + y) for k in range(1, NZL)]
    )
    scan.scatter()
    scan.totals()
    scan.give_back()
    scan.finish()


def attention_kernel(
    q_ref, k_ref, v_ref, layer_ref, gain_ref, rate_ref, len_ref, in_ref,
    px_ref, pz_ref, attention_buf, normed_buf,
):
    base = lax.axis_index("ctx") * ROWS
    bounds = doc_bounds(len_ref)
    offsets, entering, _ = edge_tables(base, bounds)
    same, distance = pair_tables(base, bounds)
    for h in range(HEADS):
        cols = pl.ds(h * WIDTH, WIDTH)
        rate = rate_ref[h]
        q, k, v = q_ref[:, cols], k_ref[:, cols], v_ref[:, cols]
        mask = jnp.where(same, jnp.exp(-rate * distance), 0.0)
        entry = jnp.where(entering, jnp.exp(-rate * offsets), 0.0)
        s_high, s_low = split(matmul(q, k, NT) * mask)
        in_high, in_low = split(in_ref[h])
        attention = matmul(s_high, v, NN) + matmul(s_low, v, NN)
        attention += entry * (matmul(q, in_high, NN) + matmul(q, in_low, NN))
        attention_buf[:, cols] = attention
    attention = attention_buf[...]
    mean = jnp.mean(attention * attention, axis=-1, keepdims=True)
    normed_buf[...] = (attention * lax.rsqrt(mean + norm_eps) * gain_ref[...]).astype(bf16)
    for h in range(HEADS):
        x, z_high = h // 2, h % 2
        product = matmul(normed_buf[:, pl.ds(h * WIDTH, WIDTH)], layer_ref[...], TN)
        for core in range(2):
            px_ref[x, z_high, core] = product[core * 64:core * 64 + 64, :XCOLS]
            for z_low in range(NZL):
                row = core * 64 + z_low * 16
                pz_ref[z_high * 4 + z_low, core, x] = product[row:row + 16, XCOLS:]


def pair_tables(base, bounds):
    rows = lax.broadcasted_iota(jnp.int32, (ROWS, ROWS), 0)
    columns = lax.broadcasted_iota(jnp.int32, (ROWS, ROWS), 1)
    same = (doc_of(base + rows, bounds) == doc_of(base + columns, bounds)) & (rows >= columns)
    return same, jnp.maximum(rows - columns, 0).astype(f32)


def gradients_kernel(
    q_ref, k_ref, v_ref, g_ref, rate_ref, len_ref, in_ref, grad_ref, dq_ref, dk_ref, dv_ref,
):
    base = lax.axis_index("ctx") * ROWS
    bounds = doc_bounds(len_ref)
    offsets, entering, leaving = edge_tables(base, bounds)
    same, distance = pair_tables(base, bounds)
    for h in range(HEADS):
        cols = pl.ds(h * WIDTH, WIDTH)
        rate = rate_ref[h]
        q, k, v, g = q_ref[:, cols], k_ref[:, cols], v_ref[:, cols], g_ref[:, cols]
        mask = jnp.where(same, jnp.exp(-rate * distance), 0.0)
        entry = jnp.where(entering, jnp.exp(-rate * offsets), 0.0)
        leave = jnp.where(leaving, jnp.exp(-rate * (ROWS - offsets)), 0.0)
        s_high, s_low = split(matmul(q, k, NT) * mask)
        d_high, d_low = split(matmul(g, v, NT) * mask)
        in_high, in_low = split(in_ref[h])
        grad_high, grad_low = split(grad_ref[h])
        dq = matmul(d_high, k, NN) + matmul(d_low, k, NN)
        dq += entry * (matmul(g, in_high, NT) + matmul(g, in_low, NT))
        dq_ref[:, cols] = dq.astype(bf16)
        dk = matmul(d_high, q, TN) + matmul(d_low, q, TN)
        dk += leave * (matmul(v, grad_high, NT) + matmul(v, grad_low, NT))
        dk_ref[:, cols] = dk.astype(bf16)
        dv = matmul(s_high, g, TN) + matmul(s_low, g, TN)
        dv += leave * (matmul(k, grad_high, NN) + matmul(k, grad_low, NN))
        dv_ref[:, cols] = dv.astype(bf16)


def reduce_kernel(
    scale, px_ref, pz_ref, pull_ref, carry_ref, out_ref, grad_ref,
    cx_buf, ax_buf, x_buf, bx_buf, xz_buf, cz_buf, az_buf, z_buf, bz_buf, zx_buf, c_buf, y_buf,
    core_send, core_recv, x_send, x_recv, xz_send, xz_recv,
    z_send, z_recv, zx_send, zx_recv, y_send, y_recv, *scratch,
):
    dp, ctx, z_low, y = place()
    x, z_high, core = dp // 4, lax.rem(dp // 2, 2), lax.rem(dp, 2)
    z = z_high * 4 + z_low
    twin = (dp + 1 - 2 * core, ctx)

    def at_x(k):
        return (lax.rem(x + k, NX) * 4 + lax.rem(dp, 4), ctx)

    def at_z(k):
        there = lax.rem(z + k, NZ)
        return (x * 4 + there // 4 * 2 + core, lax.rem(there, 4) * NY + y)

    def at_y(k):
        return (dp, ctx - y + lax.rem(y + k, NY))

    scan = Scan(-1, pull_ref, carry_ref, grad_ref, scratch[:4], scratch[4:6], scratch[6:8], scratch[8:10])
    greet(
        [twin] + [at_x(k) for k in range(1, NX)] + [at_z(k) for k in range(1, NZ)]
        + [at_y(k) for k in range(1, NY)]
    )
    core_sems = (core_send, core_recv)
    order = tuple(range(1, NX)) + (0,)
    core_copies = started(
        [send(pz_ref.at[:, 1 - core], cz_buf, core_sems, NX, twin)]
        + [
            send(px_ref.at[lax.rem(x + k, NX), :, 1 - core], cx_buf.at[k], core_sems, k, twin)
            for k in order
        ]
    )
    scan.scatter()
    core_copies[0].wait_recv()
    az_buf[...] = pz_ref[:, core] + cz_buf[...]
    z_copies = started([
        send(az_buf.at[lax.rem(z + k, NZ)], z_buf.at[k], (z_send, z_recv), k, at_z(k))
        for k in range(1, NZ)
    ])
    x_copies = []
    for k, copy in zip(order, core_copies[1:]):
        copy.wait_recv()
        ax_buf[k] = px_ref[lax.rem(x + k, NX), :, core] + cx_buf[k]
        if k:
            x_copies += started([send(ax_buf.at[k], x_buf.at[k], (x_send, x_recv), k, at_x(k))])

    def gather(total, copies, buf):
        for k, copy in enumerate(copies, 1):
            copy.wait_recv()
            total = total + buf[k]
        return total

    bx_buf[...] = gather(ax_buf[0], x_copies, x_buf).reshape(bx_buf.shape)
    xz_copies = started([
        send(bx_buf.at[lax.rem(z + k, NZ)], xz_buf.at[k], (xz_send, xz_recv), k, at_z(k))
        for k in range(1, NZ)
    ])
    bz_buf[...] = gather(az_buf[z], z_copies, z_buf)
    zx_copies = started([
        send(bz_buf.at[lax.rem(x + k, NX)], zx_buf.at[k], (zx_send, zx_recv), k, at_x(k))
        for k in range(1, NX)
    ])
    scan.totals()
    scan.give_back()
    right = gather(bz_buf[x], zx_copies, zx_buf)
    left = gather(bx_buf[z], xz_copies, xz_buf)
    for j in range(NY):
        c_buf[j, :, :XCOLS] = left[2 * j:2 * j + 2, :]
        c_buf[j, :, XCOLS:] = right[2 * j:2 * j + 2, :]
    y_copies = started([
        send(c_buf.at[lax.rem(y + k, NY)], y_buf.at[k], (y_send, y_recv), k, at_y(k))
        for k in range(1, NY)
    ])
    out_ref[...] = gather(c_buf[y], y_copies, y_buf) * scale
    scan.finish()
    for copy in core_copies + x_copies + z_copies + xz_copies + zx_copies + y_copies:
        copy.wait_send()


def on_device(queries, keys, values, out_grad, layer_grad, norm_gain, decay_rates, doc_lengths):
    rows, features, bucket = ROWS, HEADS * WIDTH, layer_grad.shape[2]
    scale = 1.0 / math.sqrt(rows * lax.axis_size("dp") * lax.axis_size("ctx"))
    q, k, v, g = (a.reshape(rows, features) for a in (queries, keys, values, out_grad))
    layer = layer_grad.reshape(rows, bucket)
    states = jax.ShapeDtypeStruct((HEADS, WIDTH, WIDTH), f32)
    state, pull, carry = pl.pallas_call(
        summary_kernel,
        out_shape=(states, states, jax.ShapeDtypeStruct((16, WIDTH), f32)),
        in_specs=[VMEM_SPEC] * 4 + [SMEM_SPEC] * 2,
        out_specs=(VMEM_SPEC,) * 3,
        name="summary",
    )(q, k, v, g, decay_rates, doc_lengths)
    state_in = pl.pallas_call(
        scan_kernel,
        out_shape=states,
        in_specs=[VMEM_SPEC] * 2,
        out_specs=VMEM_SPEC,
        scratch_shapes=SCAN_BUFS + SCAN_SEMS,
        compiler_params=pltpu.CompilerParams(collective_id=0, has_side_effects=True),
        name="scan",
    )(state, carry)
    zcols = bucket - XCOLS
    product_shapes = (
        jax.ShapeDtypeStruct((NX, 2, 2, 64, XCOLS), f32),
        jax.ShapeDtypeStruct((NZ, 2, NX, 16, zcols), f32),
    )
    px, pz = pl.pallas_call(
        attention_kernel,
        out_shape=product_shapes,
        in_specs=[VMEM_SPEC] * 5 + [SMEM_SPEC] * 2 + [VMEM_SPEC],
        out_specs=(VMEM_SPEC,) * 2,
        scratch_shapes=[pltpu.VMEM((rows, features), f32), pltpu.VMEM((rows, features), bf16)],
        name="attention",
    )(q, k, v, layer, norm_gain.reshape(1, features), decay_rates, doc_lengths, state_in)
    dma = pltpu.SemaphoreType.DMA
    proj_grad, state_grad = pl.pallas_call(
        functools.partial(reduce_kernel, scale),
        out_shape=(jax.ShapeDtypeStruct((2, bucket), f32), states),
        in_specs=[VMEM_SPEC] * 4,
        out_specs=(VMEM_SPEC,) * 2,
        scratch_shapes=[pltpu.VMEM((NX, 2, 64, XCOLS), f32)] * 3
        + [pltpu.VMEM((NZ, 16, XCOLS), f32)] * 2
        + [pltpu.VMEM((NZ, NX, 16, zcols), f32)] * 3
        + [pltpu.VMEM((NX, 16, zcols), f32)] * 2
        + [pltpu.VMEM((NY, 2, bucket), f32)] * 2
        + [dma((NX + 1,))] * 2 + [dma((NX,))] * 2 + [dma((NZ,))] * 4
        + [dma((NX,))] * 2 + [dma((NY,))] * 2
        + SCAN_BUFS + SCAN_SEMS,
        compiler_params=pltpu.CompilerParams(collective_id=1, has_side_effects=True),
        name="reduce",
    )(px, pz, pull, carry)
    grad_shape = jax.ShapeDtypeStruct((rows, features), bf16)
    query_grad, key_grad, value_grad = pl.pallas_call(
        gradients_kernel,
        out_shape=(grad_shape,) * 3,
        in_specs=[VMEM_SPEC] * 4 + [SMEM_SPEC] * 2 + [VMEM_SPEC] * 2,
        out_specs=(VMEM_SPEC,) * 3,
        name="gradients",
    )(q, k, v, g, decay_rates, doc_lengths, state_in, state_grad)
    shape_out = (1, rows, features)
    return (
        query_grad.reshape(shape_out),
        key_grad.reshape(shape_out),
        value_grad.reshape(shape_out),
        proj_grad,
    )


def solution(mesh):
    block = P("dp", "ctx", None)
    return jax.shard_map(
        on_device,
        mesh=mesh,
        in_specs=(block,) * 5 + (P(), P(), P("dp", None)),
        out_specs=(block,) * 3 + (P(("dp", "ctx"), None),),
        check_vma=False,
    )
```

time: 122 us -> 113 us (0.926); the launches traced: 121 us -> 111 us
  Pallas kernels: 119 us -> 110 us
    pallas_call x3 -> x4, Pallas kernels: 117 us -> 107 us  [the longest x1 60.9 us: on_device(): pl.pallas_call(functools.partial(reduce_kernel, scale), out_shape=(jax.Sh...]
where the time goes in v2:
time: 113 us; the launch traced here: 111 us
  Pallas kernels  110 us (97%)
    pallas_call x1, Pallas kernels, on_device(): pl.pallas_call(functools.partial(reduce_kernel, scale), out_shape=(jax.Sh...  60.9 us
    pallas_call x1, Pallas kernels, on_device(): pl.pallas_call(scan_kernel, out_shape=states, in_specs=[VMEM_SPEC] * 2, o...  35.8 us
    pallas_call x1, Pallas kernels, on_device(): pl.pallas_call(attention_kernel, out_shape=product_shapes, in_specs=[VMEM...  5.29 us
    pallas_call x1, Pallas kernels, on_device(): pl.pallas_call(gradients_kernel, out_shape=(grad_shape,) * 3, in_specs=[V...  5 us
    pallas_call x1, Pallas kernels, on_device(): pl.pallas_call(summary_kernel, out_shape=(states, states, jax.ShapeDtypeS...  2.82 us

profile of v2, /device:TPU:1, one launch (start us, length us, event | category | flops | bytes accessed | tf_op | source)
XLA Modules:
  0.0 111.0 jit_solution(8603953897189420396)
XLA Ops:
  0.6 2.8 %summary.1 = (f32[8,128,128]{2,1,0:T(8,128)}, f32[8,128,128]{2,1,0:T(8,128)}, f32[16,128]{1,0:T(8,128)}) custom-call(bf16[128,1024]{1,0:T(8,128)(2,1)} %bitcast.9, bf16[128,1024]{1,0:T(8,128)(2,1)} %bitcast.12, bf16[128,1024]{1,0:T(8,128)(2,1)} %bitcast.15, bf16[128,1024]{1,0:T(8,128)(2,1)} %bitcast.18, f32[8]{0:T(128)} %rate_ref.5, s32[1,4]{1,0:T(1,128)} %len_ref.5), custom_call_target="tpu_custom_call" | custom-call | tf_op jit(solution)/shard_map/summary/pallas_call | solution.py:357
  3.4 35.8 %scan.1.in_ref = f32[8,128,128]{2,1,0:T(8,128)} custom-call(f32[8,128,128]{2,1,0:T(8,128)} %get-tuple-element.14.state_ref, f32[16,128]{1,0:T(8,128)} %get-tuple-element.15.carry_ref), custom_call_target="tpu_custom_call" | custom-call | tf_op jit(solution)/shard_map/scan/pallas_call | solution.py:364
  39.2 5.3 %attention.1 = (f32[4,2,2,64,512]{4,3,2,1,0:T(8,128)}, f32[8,2,4,16,256]{4,3,2,1,0:T(8,128)}) custom-call(bf16[128,1024]{1,0:T(8,128)(2,1)} %bitcast.10, bf16[128,1024]{1,0:T(8,128)(2,1)} %bitcast.13, bf16[128,1024]{1,0:T(8,128)(2,1)} %bitcast.16, bf16[128,768]{1,0:T(8,128)(2,1)} %bitcast.20, f32[1,1024]{1,0:T(1,128)} %bitcast.21, f32[8]{0:T(128)} %rate_ref.5, ...), custom_call_target="tpu_custom_call" | custom-call | tf_op jit(solution)/shard_map/attention/pallas_call | solution.py:378
  44.5 60.9 %reduce.1 = (f32[2,768]{1,0:T(2,128)}, f32[8,128,128]{2,1,0:T(8,128)}) custom-call(f32[4,2,2,64,512]{4,3,2,1,0:T(8,128)} %get-tuple-element.16.px_ref, f32[8,2,4,16,256]{4,3,2,1,0:T(8,128)} %get-tuple-element.17.pz_ref, f32[8,128,128]{2,1,0:T(8,128)} %get-tuple-element.18.pull_ref, f32[16,128]{1,0:T(8,128)} %get-tuple-element.15.carry_ref), custom_call_target="tpu_custom_call" | custom-call | tf_op jit(solution)/shard_map/reduce/pallas_call | solution.py:387
  105.4 0.0 copy-start
  105.4 5.0 %gradients.1 = (bf16[128,1024]{1,0:T(8,128)(2,1)}, bf16[128,1024]{1,0:T(8,128)(2,1)}, bf16[128,1024]{1,0:T(8,128)(2,1)}) custom-call(bf16[128,1024]{1,0:T(8,128)(2,1)} %bitcast.11, bf16[128,1024]{1,0:T(8,128)(2,1)} %bitcast.14, bf16[128,1024]{1,0:T(8,128)(2,1)} %bitcast.17, bf16[128,1024]{1,0:T(8,128)(2,1)} %bitcast.19, f32[8]{0:T(128)} %rate_ref.5, ...), custom_call_target="tpu_custom_call" | custom-call | tf_op jit(solution)/shard_map/gradients/pallas_call | solution.py:404
  110.4 0.0 copy-done
  110.4 0.6 copy.13
Async XLA Ops:
  105.4 5.0 %copy-start = (f32[2,768]{1,0:T(2,128)S(1)}, f32[2,768]{1,0:T(2,128)}, u32[]{:S(2)}) copy-start(f32[2,768]{1,0:T(2,128)} %get-tuple-element.31) | copy-start | bytes 18436

commit v3 on v2

--- a/solution.py
+++ b/solution.py
@@ -106,6 +106,7 @@
         self.buf, self.back, self.total, self.group = bufs
         self.out_sems, self.back_sems, self.group_sems = out_sems, back_sems, group_sems
         self.dp, _, self.z, self.y = place()
+        self.out_copies = []
         self.order = range(NY) if step > 0 else range(NY - 1, -1, -1)
 
     def at_y(self, k):
@@ -117,12 +118,11 @@
     def block(self, j):
         return self.buf[lax.rem(self.y - j + NY, NY)]
 
-    def scatter(self):
-        self.out_copies = started([
+    def scatter(self, offsets):
+        self.out_copies += started([
             send(self.src.at[lax.rem(self.y + k, NY)], self.buf.at[k], self.out_sems, k, self.at_y(k))
-            for k in range(1, NY)
+            for k in offsets
         ])
-        self.buf[0] = self.src[self.y]
 
     def group_copy(self, far):
         there = (self.dp, (self.z + self.step * far) * NY + self.y)
@@ -133,6 +133,7 @@
         return (other >= 0) & (other < NZL)
 
     def totals(self):
+        self.buf[0] = self.src[self.y]
         for copy in self.out_copies:
             copy.wait_recv()
         total = jnp.zeros((WIDTH, WIDTH), f32)
@@ -161,12 +162,14 @@
         ])
         self.result[self.y] = self.back[self.y]
 
-    def finish(self):
+    def arrive(self):
         for k in range(1, NY):
             send(
                 self.back.at[0], self.result.at[lax.rem(self.y - k + NY, NY)],
                 self.back_sems, k, self.at_y(k),
             ).wait_recv()
+
+    def finish(self):
         for far in (1, 2):
             pl.when(self.has(self.step * far))(lambda far=far: self.group_copy(far).wait_send())
         for copy in self.out_copies + self.back_copies:
@@ -185,20 +188,7 @@
     pl.semaphore_wait(barrier, len(devices))
 
 
-def scan_kernel(state_ref, carry_ref, in_ref, *scratch):
-    dp, ctx, z, y = place()
-    scan = Scan(1, state_ref, carry_ref, in_ref, scratch[:4], scratch[4:6], scratch[6:8], scratch[8:10])
-    greet(
-        [scan.at_y(k) for k in range(1, NY)]
-        + [(dp, lax.rem(z + k, NZL) * NY + y) for k in range(1, NZL)]
-    )
-    scan.scatter()
-    scan.totals()
-    scan.give_back()
-    scan.finish()
-
-
-def attention_kernel(
+def attention_part(
     q_ref, k_ref, v_ref, layer_ref, gain_ref, rate_ref, len_ref, in_ref,
     px_ref, pz_ref, attention_buf, normed_buf,
 ):
@@ -237,12 +227,10 @@
     return same, jnp.maximum(rows - columns, 0).astype(f32)
 
 
-def gradients_kernel(
-    q_ref, k_ref, v_ref, g_ref, rate_ref, len_ref, in_ref, grad_ref, dq_ref, dk_ref, dv_ref,
-):
+def block_part(q_ref, k_ref, v_ref, g_ref, rate_ref, len_ref, in_ref, dq_ref, dk_ref, dv_ref):
     base = lax.axis_index("ctx") * ROWS
     bounds = doc_bounds(len_ref)
-    offsets, entering, leaving = edge_tables(base, bounds)
+    offsets, entering, _ = edge_tables(base, bounds)
     same, distance = pair_tables(base, bounds)
     for h in range(HEADS):
         cols = pl.ds(h * WIDTH, WIDTH)
@@ -250,25 +238,37 @@
         q, k, v, g = q_ref[:, cols], k_ref[:, cols], v_ref[:, cols], g_ref[:, cols]
         mask = jnp.where(same, jnp.exp(-rate * distance), 0.0)
         entry = jnp.where(entering, jnp.exp(-rate * offsets), 0.0)
-        leave = jnp.where(leaving, jnp.exp(-rate * (ROWS - offsets)), 0.0)
         s_high, s_low = split(matmul(q, k, NT) * mask)
         d_high, d_low = split(matmul(g, v, NT) * mask)
         in_high, in_low = split(in_ref[h])
-        grad_high, grad_low = split(grad_ref[h])
         dq = matmul(d_high, k, NN) + matmul(d_low, k, NN)
         dq += entry * (matmul(g, in_high, NT) + matmul(g, in_low, NT))
         dq_ref[:, cols] = dq.astype(bf16)
-        dk = matmul(d_high, q, TN) + matmul(d_low, q, TN)
-        dk += leave * (matmul(v, grad_high, NT) + matmul(v, grad_low, NT))
-        dk_ref[:, cols] = dk.astype(bf16)
-        dv = matmul(s_high, g, TN) + matmul(s_low, g, TN)
-        dv += leave * (matmul(k, grad_high, NN) + matmul(k, grad_low, NN))
-        dv_ref[:, cols] = dv.astype(bf16)
-
-
-def reduce_kernel(
-    scale, px_ref, pz_ref, pull_ref, carry_ref, out_ref, grad_ref,
-    cx_buf, ax_buf, x_buf, bx_buf, xz_buf, cz_buf, az_buf, z_buf, bz_buf, zx_buf, c_buf, y_buf,
+        dk_ref[:, cols] = matmul(d_high, q, TN) + matmul(d_low, q, TN)
+        dv_ref[:, cols] = matmul(s_high, g, TN) + matmul(s_low, g, TN)
+
+
+def gradients_kernel(
+    k_ref, v_ref, rate_ref, len_ref, grad_ref, dq_part, dk_part, dv_part, dq_ref, dk_ref, dv_ref,
+):
+    offsets, _, leaving = edge_tables(lax.axis_index("ctx") * ROWS, doc_bounds(len_ref))
+    dq_ref[...] = dq_part[...]
+    for h in range(HEADS):
+        cols = pl.ds(h * WIDTH, WIDTH)
+        k, v = k_ref[:, cols], v_ref[:, cols]
+        leave = jnp.where(leaving, jnp.exp(-rate_ref[h] * (ROWS - offsets)), 0.0)
+        grad_high, grad_low = split(grad_ref[h])
+        dk = leave * (matmul(v, grad_high, NT) + matmul(v, grad_low, NT))
+        dk_ref[:, cols] = (dk_part[:, cols] + dk).astype(bf16)
+        dv = leave * (matmul(k, grad_high, NN) + matmul(k, grad_low, NN))
+        dv_ref[:, cols] = (dv_part[:, cols] + dv).astype(bf16)
+
+
+def main_kernel(
+    scale, q_ref, k_ref, v_ref, g_ref, layer_ref, gain_ref, rate_ref, len_ref,
+    state_ref, pull_ref, carry_ref,
+    out_ref, grad_ref, dq_ref, dk_ref, dv_ref,
+    in_ref, px_ref, pz_ref, attention_buf, normed_buf, cx_buf, ax_buf, x_buf, bx_buf, xz_buf, cz_buf, az_buf, z_buf, bz_buf, zx_buf, c_buf, y_buf,
     core_send, core_recv, x_send, x_recv, xz_send, xz_recv,
     z_send, z_recv, zx_send, zx_recv, y_send, y_recv, *scratch,
 ):
@@ -287,10 +287,24 @@
     def at_y(k):
         return (dp, ctx - y + lax.rem(y + k, NY))
 
-    scan = Scan(-1, pull_ref, carry_ref, grad_ref, scratch[:4], scratch[4:6], scratch[6:8], scratch[8:10])
+    def scan_of(step, src, result, own):
+        return Scan(step, src, carry_ref, result, own[:4], own[4:6], own[6:8], own[8:10])
+
+    ahead = scan_of(1, state_ref, in_ref, scratch[:10])
+    scan = scan_of(-1, pull_ref, grad_ref, scratch[10:])
     greet(
         [twin] + [at_x(k) for k in range(1, NX)] + [at_z(k) for k in range(1, NZ)]
         + [at_y(k) for k in range(1, NY)]
+    )
+    ahead.scatter(range(1, NY))
+    ahead.totals()
+    scan.scatter((1, 7, 2, 6))
+    ahead.give_back()
+    scan.scatter((3, 5, 4))
+    ahead.arrive()
+    attention_part(
+        q_ref, k_ref, v_ref, layer_ref, gain_ref, rate_ref, len_ref, in_ref,
+        px_ref, pz_ref, attention_buf, normed_buf,
     )
     core_sems = (core_send, core_recv)
     order = tuple(range(1, NX)) + (0,)
@@ -301,7 +315,6 @@
             for k in order
         ]
     )
-    scan.scatter()
     core_copies[0].wait_recv()
     az_buf[...] = pz_ref[:, core] + cz_buf[...]
     z_copies = started([
@@ -315,6 +328,9 @@
         if k:
             x_copies += started([send(ax_buf.at[k], x_buf.at[k], (x_send, x_recv), k, at_x(k))])
 
+    block_part(q_ref, k_ref, v_ref, g_ref, rate_ref, len_ref, in_ref, dq_ref, dk_ref, dv_ref)
+    scan.totals()
+
     def gather(total, copies, buf):
         for k, copy in enumerate(copies, 1):
             copy.wait_recv()
@@ -326,13 +342,12 @@
         send(bx_buf.at[lax.rem(z + k, NZ)], xz_buf.at[k], (xz_send, xz_recv), k, at_z(k))
         for k in range(1, NZ)
     ])
+    scan.give_back()
     bz_buf[...] = gather(az_buf[z], z_copies, z_buf)
     zx_copies = started([
         send(bz_buf.at[lax.rem(x + k, NX)], zx_buf.at[k], (zx_send, zx_recv), k, at_x(k))
         for k in range(1, NX)
     ])
-    scan.totals()
-    scan.give_back()
     right = gather(bz_buf[x], zx_copies, zx_buf)
     left = gather(bx_buf[z], xz_copies, xz_buf)
     for j in range(NY):
@@ -343,7 +358,9 @@
         for k in range(1, NY)
     ])
     out_ref[...] = gather(c_buf[y], y_copies, y_buf) * scale
+    scan.arrive()
     scan.finish()
+    ahead.finish()
     for copy in core_copies + x_copies + z_copies + xz_copies + zx_copies + y_copies:
         copy.wait_send()
 
@@ -361,53 +378,40 @@
         out_specs=(VMEM_SPEC,) * 3,
         name="summary",
     )(q, k, v, g, decay_rates, doc_lengths)
-    state_in = pl.pallas_call(
-        scan_kernel,
-        out_shape=states,
-        in_specs=[VMEM_SPEC] * 2,
-        out_specs=VMEM_SPEC,
-        scratch_shapes=SCAN_BUFS + SCAN_SEMS,
-        compiler_params=pltpu.CompilerParams(collective_id=0, has_side_effects=True),
-        name="scan",
-    )(state, carry)
     zcols = bucket - XCOLS
-    product_shapes = (
-        jax.ShapeDtypeStruct((NX, 2, 2, 64, XCOLS), f32),
-        jax.ShapeDtypeStruct((NZ, 2, NX, 16, zcols), f32),
-    )
-    px, pz = pl.pallas_call(
-        attention_kernel,
-        out_shape=product_shapes,
-        in_specs=[VMEM_SPEC] * 5 + [SMEM_SPEC] * 2 + [VMEM_SPEC],
-        out_specs=(VMEM_SPEC,) * 2,
-        scratch_shapes=[pltpu.VMEM((rows, features), f32), pltpu.VMEM((rows, features), bf16)],
-        name="attention",
-    )(q, k, v, layer, norm_gain.reshape(1, features), decay_rates, doc_lengths, state_in)
     dma = pltpu.SemaphoreType.DMA
-    proj_grad, state_grad = pl.pallas_call(
-        functools.partial(reduce_kernel, scale),
-        out_shape=(jax.ShapeDtypeStruct((2, bucket), f32), states),
-        in_specs=[VMEM_SPEC] * 4,
-        out_specs=(VMEM_SPEC,) * 2,
-        scratch_shapes=[pltpu.VMEM((NX, 2, 64, XCOLS), f32)] * 3
+    part = jax.ShapeDtypeStruct((rows, features), f32)
+    grad_shape = jax.ShapeDtypeStruct((rows, features), bf16)
+    proj_grad, state_grad, *parts = pl.pallas_call(
+        functools.partial(main_kernel, scale),
+        out_shape=(jax.ShapeDtypeStruct((2, bucket), f32), states, grad_shape, part, part),
+        in_specs=[VMEM_SPEC] * 6 + [SMEM_SPEC] * 2 + [VMEM_SPEC] * 3,
+        out_specs=(VMEM_SPEC,) * 5,
+        scratch_shapes=[
+            HEADS_BUF,
+            pltpu.VMEM((NX, 2, 2, 64, XCOLS), f32),
+            pltpu.VMEM((NZ, 2, NX, 16, zcols), f32),
+            pltpu.VMEM((rows, features), f32),
+            pltpu.VMEM((rows, features), bf16),
+        ]
+        + [pltpu.VMEM((NX, 2, 64, XCOLS), f32)] * 3
         + [pltpu.VMEM((NZ, 16, XCOLS), f32)] * 2
         + [pltpu.VMEM((NZ, NX, 16, zcols), f32)] * 3
         + [pltpu.VMEM((NX, 16, zcols), f32)] * 2
         + [pltpu.VMEM((NY, 2, bucket), f32)] * 2
         + [dma((NX + 1,))] * 2 + [dma((NX,))] * 2 + [dma((NZ,))] * 4
         + [dma((NX,))] * 2 + [dma((NY,))] * 2
-        + SCAN_BUFS + SCAN_SEMS,
-        compiler_params=pltpu.CompilerParams(collective_id=1, has_side_effects=True),
-        name="reduce",
-    )(px, pz, pull, carry)
-    grad_shape = jax.ShapeDtypeStruct((rows, features), bf16)
+        + (SCAN_BUFS + SCAN_SEMS) * 2,
+        compiler_params=pltpu.CompilerParams(collective_id=0, has_side_effects=True),
+        name="main",
+    )(q, k, v, g, layer, norm_gain.reshape(1, features), decay_rates, doc_lengths, state, pull, carry)
     query_grad, key_grad, value_grad = pl.pallas_call(
         gradients_kernel,
         out_shape=(grad_shape,) * 3,
-        in_specs=[VMEM_SPEC] * 4 + [SMEM_SPEC] * 2 + [VMEM_SPEC] * 2,
+        in_specs=[VMEM_SPEC] * 2 + [SMEM_SPEC] * 2 + [VMEM_SPEC] * 4,
         out_specs=(VMEM_SPEC,) * 3,
         name="gradients",
-    )(q, k, v, g, decay_rates, doc_lengths, state_in, state_grad)
+    )(k, v, decay_rates, doc_lengths, state_grad, *parts)
     shape_out = (1, rows, features)
     return (
         query_grad.reshape(shape_out),

time: 113 us -> 101 us (0.89); the launches traced: 111 us -> 100 us
  Pallas kernels: 110 us -> 98.5 us
    pallas_call x3 -> x1, Pallas kernels: 102 us -> 92.7 us  [on_device(): pl.pallas_call(functools.partial(main_kernel, scale), out_shape=(jax.Shap...]
    pallas_call x1, Pallas kernels: 5 us -> 3.06 us  [on_device(): pl.pallas_call(gradients_kernel, out_shape=(grad_shape,) * 3, in_specs=[V...]
where the time goes in v3:
time: 101 us; the launch traced here: 100 us
  Pallas kernels  98.5 us (98%)
  local copies, waits for them, and re-layouts  1.28 us (1%)
    pallas_call x1, Pallas kernels, on_device(): pl.pallas_call(functools.partial(main_kernel, scale), out_shape=(jax.Shap...  92.7 us
    pallas_call x1, Pallas kernels, on_device(): pl.pallas_call(gradients_kernel, out_shape=(grad_shape,) * 3, in_specs=[V...  3.06 us
    pallas_call x1, Pallas kernels, on_device(): pl.pallas_call(summary_kernel, out_shape=(states, states, jax.ShapeDtypeS...  2.79 us

profile of v3, /device:TPU:1, one launch (start us, length us, event | category | flops | bytes accessed | tf_op | source)
XLA Modules:
  0.0 100.4 jit_solution(13580636312946381005)
XLA Ops:
  0.6 2.8 %summary.1 = (f32[8,128,128]{2,1,0:T(8,128)}, f32[8,128,128]{2,1,0:T(8,128)}, f32[16,128]{1,0:T(8,128)}) custom-call(bf16[128,1024]{1,0:T(8,128)(2,1)} %bitcast.15, bf16[128,1024]{1,0:T(8,128)(2,1)} %bitcast.9, bf16[128,1024]{1,0:T(8,128)(2,1)} %bitcast.12, bf16[128,1024]{1,0:T(8,128)(2,1)} %bitcast.17, f32[8]{0:T(128)} %rate_ref.5, s32[1,4]{1,0:T(1,128)} %len_ref.5), custom_call_target="tpu_custom_call" | custom-call | tf_op jit(solution)/shard_map/summary/pallas_call | solution.py:374
  3.4 92.7 %main.1 = (f32[2,768]{1,0:T(2,128)}, f32[8,128,128]{2,1,0:T(8,128)}, bf16[128,1024]{1,0:T(8,128)(2,1)}, f32[128,1024]{1,0:T(8,128)}, f32[128,1024]{1,0:T(8,128)}) custom-call(bf16[128,1024]{1,0:T(8,128)(2,1)} %bitcast.16, bf16[128,1024]{1,0:T(8,128)(2,1)} %bitcast.10, bf16[128,1024]{1,0:T(8,128)(2,1)} %bitcast.13, bf16[128,1024]{1,0:T(8,128)(2,1)} %bitcast.18, ...), custom_call_target="tpu_custom_call" | custom-call | tf_op jit(solution)/shard_map/main/pallas_call | solution.py:385
  96.1 3.1 %gradients.1 = (bf16[128,1024]{1,0:T(8,128)(2,1)}, bf16[128,1024]{1,0:T(8,128)(2,1)}, bf16[128,1024]{1,0:T(8,128)(2,1)}) custom-call(bf16[128,1024]{1,0:T(8,128)(2,1)} %bitcast.11, bf16[128,1024]{1,0:T(8,128)(2,1)} %bitcast.14, f32[8]{0:T(128)} %rate_ref.5, s32[1,4]{1,0:T(1,128)} %len_ref.5, f32[8,128,128]{2,1,0:T(8,128)} %get-tuple-element.18.grad_ref, ...), custom_call_target="tpu_custom_call" | custom-call | tf_op jit(solution)/shard_map/gradients/pallas_call | solution.py:408
  99.1 0.0 copy-start
  99.1 0.7 copy-done
  99.8 0.6 copy.13
Async XLA Ops:
  99.1 0.7 copy-start

commit v4 on v3

--- a/solution.py
+++ b/solution.py
@@ -52,21 +52,16 @@
     return offsets.astype(f32), entering, leaving
 
 
-def summary_kernel(q_ref, k_ref, v_ref, g_ref, rate_ref, len_ref, state_ref, pull_ref, carry_ref):
+def state_part(k_ref, v_ref, rate_ref, len_ref, state_ref, carry_ref):
     ctx = lax.axis_index("ctx")
     bounds = doc_bounds(len_ref)
-    offsets, entering, leaving = edge_tables(ctx * ROWS, bounds)
+    offsets, _, leaving = edge_tables(ctx * ROWS, bounds)
     for h in range(HEADS):
         cols = pl.ds(h * WIDTH, WIDTH)
-        rate = rate_ref[h]
-        entry = jnp.where(entering, jnp.exp(-rate * offsets), 0.0)
-        leave = jnp.where(leaving, jnp.exp(-rate * (ROWS - offsets)), 0.0)
+        leave = jnp.where(leaving, jnp.exp(-rate_ref[h] * (ROWS - offsets)), 0.0)
         high, low = split(k_ref[:, cols].astype(f32) * leave)
         v = v_ref[:, cols]
         state_ref[h] = matmul(high, v, TN) + matmul(low, v, TN)
-        high, low = split(q_ref[:, cols].astype(f32) * entry)
-        g = g_ref[:, cols]
-        pull_ref[h] = matmul(high, g, TN) + matmul(low, g, TN)
     group, own = ctx // NY, lax.rem(ctx, NY)
     rate = rate_ref[own]
 
@@ -82,6 +77,16 @@
     carry_ref[pl.ds(9, 1), :] = carry((group + 1) * NY, NY)
 
 
+def pull_part(q_ref, g_ref, rate_ref, len_ref, pull_ref):
+    offsets, entering, _ = edge_tables(lax.axis_index("ctx") * ROWS, doc_bounds(len_ref))
+    for h in range(HEADS):
+        cols = pl.ds(h * WIDTH, WIDTH)
+        entry = jnp.where(entering, jnp.exp(-rate_ref[h] * offsets), 0.0)
+        high, low = split(q_ref[:, cols].astype(f32) * entry)
+        g = g_ref[:, cols]
+        pull_ref[h] = matmul(high, g, TN) + matmul(low, g, TN)
+
+
 def place():
     dp, ctx = lax.axis_index("dp"), lax.axis_index("ctx")
     return dp, ctx, ctx // NY, lax.rem(ctx, NY)
@@ -100,17 +105,25 @@
     return copies
 
 
+HALF = WIDTH // 2
+SIDES = ((1, 3, 0), (NY - 1, NY - 3, HALF))
+
+
 class Scan:
-    def __init__(self, step, src, carry, result, bufs, out_sems, back_sems, group_sems):
+    def __init__(self, step, src, carry, result, scratch):
         self.step, self.src, self.carry_ref, self.result = step, src, carry, result
-        self.buf, self.back, self.total, self.group = bufs
-        self.out_sems, self.back_sems, self.group_sems = out_sems, back_sems, group_sems
+        self.buf, self.back, self.total, self.group, self.relay = scratch[:5]
+        sems = [scratch[i:i + 2] for i in range(5, 15, 2)]
+        self.out_sems, self.back_sems, self.near_sems, self.far_sems, self.group_sems = sems
         self.dp, _, self.z, self.y = place()
-        self.out_copies = []
+        self.out_copies, self.back_copies, self.relay_copies = [], [], []
         self.order = range(NY) if step > 0 else range(NY - 1, -1, -1)
 
+    def around(self, k):
+        return lax.rem(self.y + k, NY)
+
     def at_y(self, k):
-        return (self.dp, self.z * NY + lax.rem(self.y + k, NY))
+        return (self.dp, self.z * NY + self.around(k))
 
     def carry(self, j):
         return self.carry_ref[pl.ds(j, 1), :]
@@ -118,9 +131,35 @@
     def block(self, j):
         return self.buf[lax.rem(self.y - j + NY, NY)]
 
+    def half_way(self, phase):
+        src = (self.src, self.back)[phase].at[self.around(NY // 2)]
+        for side, (near, _, row) in enumerate(SIDES):
+            at = 2 * phase + side
+            self.relay_copies += started([
+                send(src.at[pl.ds(row, HALF)], self.relay.at[at], self.near_sems, at, self.at_y(near))
+            ])
+
+    def pass_on(self, phase):
+        for copy in self.relay_copies[-2:]:
+            copy.wait_recv()
+        for side, (near, far, row) in enumerate(SIDES):
+            at = 2 * phase + side
+            slot = self.result.at[self.around(NY - near)] if phase else self.buf.at[NY // 2]
+            self.relay_copies += started([
+                send(self.relay.at[at], slot.at[pl.ds(row, HALF)], self.far_sems, at, self.at_y(far))
+            ])
+
+    def half_way_arrived(self, phase):
+        for side, (_, far, row) in enumerate(SIDES):
+            at = 2 * phase + side
+            slot = self.result.at[self.around(NY // 2)] if phase else self.buf.at[NY // 2]
+            send(
+                self.relay.at[at], slot.at[pl.ds(row, HALF)], self.far_sems, at, self.at_y(far)
+            ).wait_recv()
+
     def scatter(self, offsets):
         self.out_copies += started([
-            send(self.src.at[lax.rem(self.y + k, NY)], self.buf.at[k], self.out_sems, k, self.at_y(k))
+            send(self.src.at[self.around(k)], self.buf.at[k], self.out_sems, k, self.at_y(k))
             for k in offsets
         ])
 
@@ -136,6 +175,7 @@
         self.buf[0] = self.src[self.y]
         for copy in self.out_copies:
             copy.wait_recv()
+        self.half_way_arrived(0)
         total = jnp.zeros((WIDTH, WIDTH), f32)
         for j in self.order:
             total = self.carry(j) * total + self.block(j)
@@ -143,7 +183,7 @@
         for far in (1, 2):
             pl.when(self.has(self.step * far))(lambda far=far: self.group_copy(far).start())
 
-    def give_back(self):
+    def combine(self):
         for far in (1, 2):
             source = self.has(-self.step * far)
             pl.when(source)(lambda far=far: self.group_copy(far).wait_recv())
@@ -156,36 +196,35 @@
         for j in self.order:
             self.back[j] = now
             now = self.carry(j) * now + self.block(j)
-        self.back_copies = started([
-            send(self.back.at[lax.rem(self.y + k, NY)], self.result.at[self.y], self.back_sems, k, self.at_y(k))
-            for k in range(1, NY)
+
+    def give_back(self, offsets):
+        self.back_copies += started([
+            send(self.back.at[self.around(k)], self.result.at[self.y], self.back_sems, k, self.at_y(k))
+            for k in offsets
         ])
+
+    def arrive(self):
         self.result[self.y] = self.back[self.y]
-
-    def arrive(self):
-        for k in range(1, NY):
+        for k in DIRECT:
             send(
-                self.back.at[0], self.result.at[lax.rem(self.y - k + NY, NY)],
-                self.back_sems, k, self.at_y(k),
+                self.back.at[0], self.result.at[self.around(NY - k)], self.back_sems, k, self.at_y(k)
             ).wait_recv()
+        self.half_way_arrived(1)
 
     def finish(self):
         for far in (1, 2):
             pl.when(self.has(self.step * far))(lambda far=far: self.group_copy(far).wait_send())
-        for copy in self.out_copies + self.back_copies:
+        for copy in self.out_copies + self.back_copies + self.relay_copies:
             copy.wait_send()
 
 
+FAR, NEAR = (3, 5), (2, 6, 1, 7)
+DIRECT = FAR + NEAR
 HEADS_BUF = pltpu.VMEM((HEADS, WIDTH, WIDTH), f32)
-SCAN_BUFS = [HEADS_BUF, HEADS_BUF, pltpu.VMEM((WIDTH, WIDTH), f32), pltpu.VMEM((2, WIDTH, WIDTH), f32)]
-SCAN_SEMS = [pltpu.SemaphoreType.DMA((NY,))] * 4 + [pltpu.SemaphoreType.DMA((2,))] * 2
-
-
-def greet(devices):
-    barrier = pltpu.get_barrier_semaphore()
-    for device in devices:
-        pl.semaphore_signal(barrier, inc=1, device_id=device, device_id_type=MESH)
-    pl.semaphore_wait(barrier, len(devices))
+SCAN_SCRATCH = [
+    HEADS_BUF, HEADS_BUF, pltpu.VMEM((WIDTH, WIDTH), f32), pltpu.VMEM((2, WIDTH, WIDTH), f32),
+    pltpu.VMEM((4, HALF, WIDTH), f32),
+] + [pltpu.SemaphoreType.DMA((NY,))] * 4 + [pltpu.SemaphoreType.DMA((4,))] * 4 + [pltpu.SemaphoreType.DMA((2,))] * 2
 
 
 def attention_part(
@@ -266,9 +305,8 @@
 
 def main_kernel(
     scale, q_ref, k_ref, v_ref, g_ref, layer_ref, gain_ref, rate_ref, len_ref,
-    state_ref, pull_ref, carry_ref,
     out_ref, grad_ref, dq_ref, dk_ref, dv_ref,
-    in_ref, px_ref, pz_ref, attention_buf, normed_buf, cx_buf, ax_buf, x_buf, bx_buf, xz_buf, cz_buf, az_buf, z_buf, bz_buf, zx_buf, c_buf, y_buf,
+    state_ref, pull_ref, carry_ref, in_ref, px_ref, pz_ref, attention_buf, normed_buf, cx_buf, ax_buf, x_buf, bx_buf, xz_buf, cz_buf, az_buf, z_buf, bz_buf, zx_buf, c_buf, y_buf,
     core_send, core_recv, x_send, x_recv, xz_send, xz_recv,
     z_send, z_recv, zx_send, zx_recv, y_send, y_recv, *scratch,
 ):
@@ -287,20 +325,30 @@
     def at_y(k):
         return (dp, ctx - y + lax.rem(y + k, NY))
 
-    def scan_of(step, src, result, own):
-        return Scan(step, src, carry_ref, result, own[:4], own[4:6], own[6:8], own[8:10])
-
-    ahead = scan_of(1, state_ref, in_ref, scratch[:10])
-    scan = scan_of(-1, pull_ref, grad_ref, scratch[10:])
-    greet(
+    ahead = Scan(1, state_ref, carry_ref, in_ref, scratch[:15])
+    scan = Scan(-1, pull_ref, carry_ref, grad_ref, scratch[15:])
+    partners = (
         [twin] + [at_x(k) for k in range(1, NX)] + [at_z(k) for k in range(1, NZ)]
         + [at_y(k) for k in range(1, NY)]
     )
-    ahead.scatter(range(1, NY))
+    barrier = pltpu.get_barrier_semaphore()
+    for device in partners:
+        pl.semaphore_signal(barrier, inc=1, device_id=device, device_id_type=MESH)
+    state_part(k_ref, v_ref, rate_ref, len_ref, state_ref, carry_ref)
+    pl.semaphore_wait(barrier, len(partners))
+    ahead.half_way(0)
+    ahead.scatter(DIRECT)
+    pull_part(q_ref, g_ref, rate_ref, len_ref, pull_ref)
+    ahead.pass_on(0)
     ahead.totals()
-    scan.scatter((1, 7, 2, 6))
-    ahead.give_back()
-    scan.scatter((3, 5, 4))
+    scan.half_way(0)
+    scan.scatter(NEAR)
+    ahead.combine()
+    ahead.half_way(1)
+    ahead.give_back(DIRECT)
+    scan.pass_on(0)
+    ahead.pass_on(1)
+    scan.scatter(FAR)
     ahead.arrive()
     attention_part(
         q_ref, k_ref, v_ref, layer_ref, gain_ref, rate_ref, len_ref, in_ref,
@@ -342,12 +390,15 @@
         send(bx_buf.at[lax.rem(z + k, NZ)], xz_buf.at[k], (xz_send, xz_recv), k, at_z(k))
         for k in range(1, NZ)
     ])
-    scan.give_back()
+    scan.combine()
+    scan.half_way(1)
+    scan.give_back(FAR)
     bz_buf[...] = gather(az_buf[z], z_copies, z_buf)
     zx_copies = started([
         send(bz_buf.at[lax.rem(x + k, NX)], zx_buf.at[k], (zx_send, zx_recv), k, at_x(k))
         for k in range(1, NX)
     ])
+    scan.pass_on(1)
     right = gather(bz_buf[x], zx_copies, zx_buf)
     left = gather(bx_buf[z], xz_copies, xz_buf)
     for j in range(NY):
@@ -357,6 +408,7 @@
         send(c_buf.at[lax.rem(y + k, NY)], y_buf.at[k], (y_send, y_recv), k, at_y(k))
         for k in range(1, NY)
     ])
+    scan.give_back(NEAR)
     out_ref[...] = gather(c_buf[y], y_copies, y_buf) * scale
     scan.arrive()
     scan.finish()
@@ -371,13 +423,6 @@
     q, k, v, g = (a.reshape(rows, features) for a in (queries, keys, values, out_grad))
     layer = layer_grad.reshape(rows, bucket)
     states = jax.ShapeDtypeStruct((HEADS, WIDTH, WIDTH), f32)
-    state, pull, carry = pl.pallas_call(
-        summary_kernel,
-        out_shape=(states, states, jax.ShapeDtypeStruct((16, WIDTH), f32)),
-        in_specs=[VMEM_SPEC] * 4 + [SMEM_SPEC] * 2,
-        out_specs=(VMEM_SPEC,) * 3,
-        name="summary",
-    )(q, k, v, g, decay_rates, doc_lengths)
     zcols = bucket - XCOLS
     dma = pltpu.SemaphoreType.DMA
     part = jax.ShapeDtypeStruct((rows, features), f32)
@@ -385,9 +430,12 @@
     proj_grad, state_grad, *parts = pl.pallas_call(
         functools.partial(main_kernel, scale),
         out_shape=(jax.ShapeDtypeStruct((2, bucket), f32), states, grad_shape, part, part),
-        in_specs=[VMEM_SPEC] * 6 + [SMEM_SPEC] * 2 + [VMEM_SPEC] * 3,
+        in_specs=[VMEM_SPEC] * 6 + [SMEM_SPEC] * 2,
         out_specs=(VMEM_SPEC,) * 5,
         scratch_shapes=[
+            HEADS_BUF,
+            HEADS_BUF,
+            pltpu.VMEM((16, WIDTH), f32),
             HEADS_BUF,
             pltpu.VMEM((NX, 2, 2, 64, XCOLS), f32),
             pltpu.VMEM((NZ, 2, NX, 16, zcols), f32),
@@ -401,10 +449,10 @@
         + [pltpu.VMEM((NY, 2, bucket), f32)] * 2
         + [dma((NX + 1,))] * 2 + [dma((NX,))] * 2 + [dma((NZ,))] * 4
         + [dma((NX,))] * 2 + [dma((NY,))] * 2
-        + (SCAN_BUFS + SCAN_SEMS) * 2,
+        + SCAN_SCRATCH * 2,
         compiler_params=pltpu.CompilerParams(collective_id=0, has_side_effects=True),
         name="main",
-    )(q, k, v, g, layer, norm_gain.reshape(1, features), decay_rates, doc_lengths, state, pull, carry)
+    )(q, k, v, g, layer, norm_gain.reshape(1, features), decay_rates, doc_lengths)
     query_grad, key_grad, value_grad = pl.pallas_call(
         gradients_kernel,
         out_shape=(grad_shape,) * 3,

time: 101 us -> 98.3 us (0.973)
  Pallas kernels: 98.5 us -> 96.2 us
    pallas_call x1 -> x0, Pallas kernels: 2.79 us -> none  [on_device(): pl.pallas_call(summary_kernel, out_shape=(states, states, jax.ShapeDtypeS...]
where the time goes in v4:
time: 98.3 us; the launch traced here: 98.1 us
  Pallas kernels  96.2 us (98%)
  local copies, waits for them, and re-layouts  1.28 us (1%)
    pallas_call x1, Pallas kernels, on_device(): pl.pallas_call(functools.partial(main_kernel, scale), out_shape=(jax.Shap...  93.1 us
    pallas_call x1, Pallas kernels, on_device(): pl.pallas_call(gradients_kernel, out_shape=(grad_shape,) * 3, in_specs=[V...  3.06 us

profile of v4, /device:TPU:1, one launch (start us, length us, event | category | flops | bytes accessed | tf_op | source)
XLA Modules:
  0.0 98.1 jit_solution(17209013042592041078)
XLA Ops:
  0.6 93.1 %main.1 = (f32[2,768]{1,0:T(2,128)}, f32[8,128,128]{2,1,0:T(8,128)}, bf16[128,1024]{1,0:T(8,128)(2,1)}, f32[128,1024]{1,0:T(8,128)}, f32[128,1024]{1,0:T(8,128)}) custom-call(bf16[128,1024]{1,0:T(8,128)(2,1)} %bitcast.13, bf16[128,1024]{1,0:T(8,128)(2,1)} %bitcast.9, bf16[128,1024]{1,0:T(8,128)(2,1)} %bitcast.11, bf16[128,1024]{1,0:T(8,128)(2,1)} %bitcast.14, ...), custom_call_target="tpu_custom_call" | custom-call | tf_op jit(solution)/shard_map/main/pallas_call | solution.py:430
  93.7 3.1 %gradients.1 = (bf16[128,1024]{1,0:T(8,128)(2,1)}, bf16[128,1024]{1,0:T(8,128)(2,1)}, bf16[128,1024]{1,0:T(8,128)(2,1)}) custom-call(bf16[128,1024]{1,0:T(8,128)(2,1)} %bitcast.10, bf16[128,1024]{1,0:T(8,128)(2,1)} %bitcast.12, f32[8]{0:T(128)} %rate_ref.3, s32[1,4]{1,0:T(1,128)} %len_ref.3, f32[8,128,128]{2,1,0:T(8,128)} %get-tuple-element.12.grad_ref, ...), custom_call_target="tpu_custom_call" | custom-call | tf_op jit(solution)/shard_map/gradients/pallas_call | solution.py:456
  96.8 0.0 copy-start
  96.8 0.7 copy-done
  97.5 0.6 copy.13
Async XLA Ops:
  96.8 0.7 copy-start

commit v5 on v4

--- a/solution.py
+++ b/solution.py
@@ -227,36 +227,28 @@
 ] + [pltpu.SemaphoreType.DMA((NY,))] * 4 + [pltpu.SemaphoreType.DMA((4,))] * 4 + [pltpu.SemaphoreType.DMA((2,))] * 2
 
 
-def attention_part(
-    q_ref, k_ref, v_ref, layer_ref, gain_ref, rate_ref, len_ref, in_ref,
-    px_ref, pz_ref, attention_buf, normed_buf,
-):
+def attention_block(q_ref, k_ref, v_ref, rate_ref, len_ref, attention_buf):
     base = lax.axis_index("ctx") * ROWS
-    bounds = doc_bounds(len_ref)
-    offsets, entering, _ = edge_tables(base, bounds)
-    same, distance = pair_tables(base, bounds)
-    for h in range(HEADS):
-        cols = pl.ds(h * WIDTH, WIDTH)
-        rate = rate_ref[h]
-        q, k, v = q_ref[:, cols], k_ref[:, cols], v_ref[:, cols]
-        mask = jnp.where(same, jnp.exp(-rate * distance), 0.0)
-        entry = jnp.where(entering, jnp.exp(-rate * offsets), 0.0)
-        s_high, s_low = split(matmul(q, k, NT) * mask)
+    same, distance = pair_tables(base, doc_bounds(len_ref))
+    for h in range(HEADS):
+        cols = pl.ds(h * WIDTH, WIDTH)
+        v = v_ref[:, cols]
+        mask = jnp.where(same, jnp.exp(-rate_ref[h] * distance), 0.0)
+        s_high, s_low = split(matmul(q_ref[:, cols], k_ref[:, cols], NT) * mask)
+        attention_buf[:, cols] = matmul(s_high, v, NN) + matmul(s_low, v, NN)
+
+
+def attention_rest(q_ref, gain_ref, rate_ref, len_ref, in_ref, attention_buf, normed_buf):
+    offsets, entering, _ = edge_tables(lax.axis_index("ctx") * ROWS, doc_bounds(len_ref))
+    for h in range(HEADS):
+        cols = pl.ds(h * WIDTH, WIDTH)
+        q = q_ref[:, cols]
+        entry = jnp.where(entering, jnp.exp(-rate_ref[h] * offsets), 0.0)
         in_high, in_low = split(in_ref[h])
-        attention = matmul(s_high, v, NN) + matmul(s_low, v, NN)
-        attention += entry * (matmul(q, in_high, NN) + matmul(q, in_low, NN))
-        attention_buf[:, cols] = attention
+        attention_buf[:, cols] += entry * (matmul(q, in_high, NN) + matmul(q, in_low, NN))
     attention = attention_buf[...]
     mean = jnp.mean(attention * attention, axis=-1, keepdims=True)
     normed_buf[...] = (attention * lax.rsqrt(mean + norm_eps) * gain_ref[...]).astype(bf16)
-    for h in range(HEADS):
-        x, z_high = h // 2, h % 2
-        product = matmul(normed_buf[:, pl.ds(h * WIDTH, WIDTH)], layer_ref[...], TN)
-        for core in range(2):
-            px_ref[x, z_high, core] = product[core * 64:core * 64 + 64, :XCOLS]
-            for z_low in range(NZL):
-                row = core * 64 + z_low * 16
-                pz_ref[z_high * 4 + z_low, core, x] = product[row:row + 16, XCOLS:]
 
 
 def pair_tables(base, bounds):
@@ -340,6 +332,7 @@
     ahead.scatter(DIRECT)
     pull_part(q_ref, g_ref, rate_ref, len_ref, pull_ref)
     ahead.pass_on(0)
+    attention_block(q_ref, k_ref, v_ref, rate_ref, len_ref, attention_buf)
     ahead.totals()
     scan.half_way(0)
     scan.scatter(NEAR)
@@ -350,34 +343,57 @@
     ahead.pass_on(1)
     scan.scatter(FAR)
     ahead.arrive()
-    attention_part(
-        q_ref, k_ref, v_ref, layer_ref, gain_ref, rate_ref, len_ref, in_ref,
-        px_ref, pz_ref, attention_buf, normed_buf,
-    )
+    attention_rest(q_ref, gain_ref, rate_ref, len_ref, in_ref, attention_buf, normed_buf)
+
+    def product(block, columns):
+        features = pl.ds(pl.multiple_of(block * WIDTH, WIDTH), WIDTH)
+        return matmul(normed_buf[:, features], layer_ref[:, columns], TN)
+
+    for h in range(HEADS):
+        rows = product(h, slice(XCOLS, None))
+        for half in range(2):
+            for low in range(NZL):
+                row = half * 64 + low * 16
+                pz_ref[h % 2 * 4 + low, half, h // 2] = rows[row:row + 16]
     core_sems = (core_send, core_recv)
+    core_copies = started([send(pz_ref.at[:, 1 - core], cz_buf, core_sems, NX, twin)])
+
+    def to_twin(k):
+        there = lax.rem(x + k, NX)
+        for high in range(2):
+            rows = product(there * 2 + high, slice(0, XCOLS))
+            for half in range(2):
+                px_ref[there, high, half] = rows[half * 64:half * 64 + 64]
+        core_copies.extend(
+            started([send(px_ref.at[there, :, 1 - core], cx_buf.at[k], core_sems, k, twin)])
+        )
+
+    def to_z(offsets):
+        return started([
+            send(az_buf.at[lax.rem(z + k, NZ)], z_buf.at[k], (z_send, z_recv), k, at_z(k))
+            for k in offsets
+        ])
+
     order = tuple(range(1, NX)) + (0,)
-    core_copies = started(
-        [send(pz_ref.at[:, 1 - core], cz_buf, core_sems, NX, twin)]
-        + [
-            send(px_ref.at[lax.rem(x + k, NX), :, 1 - core], cx_buf.at[k], core_sems, k, twin)
-            for k in order
-        ]
-    )
+    for k in order[:2]:
+        to_twin(k)
     core_copies[0].wait_recv()
     az_buf[...] = pz_ref[:, core] + cz_buf[...]
-    z_copies = started([
-        send(az_buf.at[lax.rem(z + k, NZ)], z_buf.at[k], (z_send, z_recv), k, at_z(k))
-        for k in range(1, NZ)
-    ])
+    z_copies = to_z((3, 4, 5))
+    for k in order[2:]:
+        to_twin(k)
     x_copies = []
     for k, copy in zip(order, core_copies[1:]):
         copy.wait_recv()
         ax_buf[k] = px_ref[lax.rem(x + k, NX), :, core] + cx_buf[k]
         if k:
             x_copies += started([send(ax_buf.at[k], x_buf.at[k], (x_send, x_recv), k, at_x(k))])
-
+    scan.totals()
+    z_copies = to_z((1, 2)) + z_copies + to_z((6, 7))
     block_part(q_ref, k_ref, v_ref, g_ref, rate_ref, len_ref, in_ref, dq_ref, dk_ref, dv_ref)
-    scan.totals()
+    scan.combine()
+    scan.half_way(1)
+    scan.give_back(DIRECT)
 
     def gather(total, copies, buf):
         for k, copy in enumerate(copies, 1):
@@ -390,15 +406,12 @@
         send(bx_buf.at[lax.rem(z + k, NZ)], xz_buf.at[k], (xz_send, xz_recv), k, at_z(k))
         for k in range(1, NZ)
     ])
-    scan.combine()
-    scan.half_way(1)
-    scan.give_back(FAR)
+    scan.pass_on(1)
     bz_buf[...] = gather(az_buf[z], z_copies, z_buf)
     zx_copies = started([
         send(bz_buf.at[lax.rem(x + k, NX)], zx_buf.at[k], (zx_send, zx_recv), k, at_x(k))
         for k in range(1, NX)
     ])
-    scan.pass_on(1)
     right = gather(bz_buf[x], zx_copies, zx_buf)
     left = gather(bx_buf[z], xz_copies, xz_buf)
     for j in range(NY):
@@ -408,7 +421,6 @@
         send(c_buf.at[lax.rem(y + k, NY)], y_buf.at[k], (y_send, y_recv), k, at_y(k))
         for k in range(1, NY)
     ])
-    scan.give_back(NEAR)
     out_ref[...] = gather(c_buf[y], y_copies, y_buf) * scale
     scan.arrive()
     scan.finish()

time: 98.3 us -> 90.5 us (0.921)
  Pallas kernels: 96.2 us -> 88 us
    pallas_call x1, Pallas kernels: 93.1 us -> 85 us  [on_device(): pl.pallas_call(functools.partial(main_kernel, scale), out_shape=(jax.Shap...]
where the time goes in v5:
time: 90.5 us; the launch traced here: 89.9 us
  Pallas kernels  88 us (97%)
  local copies, waits for them, and re-layouts  1.28 us (1%)
    pallas_call x1, Pallas kernels, on_device(): pl.pallas_call(functools.partial(main_kernel, scale), out_shape=(jax.Shap...  85 us
    pallas_call x1, Pallas kernels, on_device(): pl.pallas_call(gradients_kernel, out_shape=(grad_shape,) * 3, in_specs=[V...  3.06 us

profile of v5, /device:TPU:1, one launch (start us, length us, event | category | flops | bytes accessed | tf_op | source)
XLA Modules:
  0.0 89.9 jit_solution(8643115119410962396)
XLA Ops:
  0.6 85.0 %main.1 = (f32[2,768]{1,0:T(2,128)}, f32[8,128,128]{2,1,0:T(8,128)}, bf16[128,1024]{1,0:T(8,128)(2,1)}, f32[128,1024]{1,0:T(8,128)}, f32[128,1024]{1,0:T(8,128)}) custom-call(bf16[128,1024]{1,0:T(8,128)(2,1)} %bitcast.13, bf16[128,1024]{1,0:T(8,128)(2,1)} %bitcast.9, bf16[128,1024]{1,0:T(8,128)(2,1)} %bitcast.11, bf16[128,1024]{1,0:T(8,128)(2,1)} %bitcast.14, ...), custom_call_target="tpu_custom_call" | custom-call | tf_op jit(solution)/shard_map/main/pallas_call | solution.py:442
  85.6 3.1 %gradients.1 = (bf16[128,1024]{1,0:T(8,128)(2,1)}, bf16[128,1024]{1,0:T(8,128)(2,1)}, bf16[128,1024]{1,0:T(8,128)(2,1)}) custom-call(bf16[128,1024]{1,0:T(8,128)(2,1)} %bitcast.10, bf16[128,1024]{1,0:T(8,128)(2,1)} %bitcast.12, f32[8]{0:T(128)} %rate_ref.3, s32[1,4]{1,0:T(1,128)} %len_ref.3, f32[8,128,128]{2,1,0:T(8,128)} %get-tuple-element.12.grad_ref, ...), custom_call_target="tpu_custom_call" | custom-call | tf_op jit(solution)/shard_map/gradients/pallas_call | solution.py:468
  88.6 0.0 copy-start
  88.7 0.7 copy-done
  89.3 0.6 copy.13
Async XLA Ops:
  88.6 0.7 copy-start

commit v6 on v5

--- a/solution.py
+++ b/solution.py
@@ -203,13 +203,16 @@
             for k in offsets
         ])
 
-    def arrive(self):
+    def arrive(self, use):
         self.result[self.y] = self.back[self.y]
+        use(self.y)
         for k in DIRECT:
             send(
                 self.back.at[0], self.result.at[self.around(NY - k)], self.back_sems, k, self.at_y(k)
             ).wait_recv()
+            use(self.around(NY - k))
         self.half_way_arrived(1)
+        use(self.around(NY // 2))
 
     def finish(self):
         for far in (1, 2):
@@ -238,17 +241,40 @@
         attention_buf[:, cols] = matmul(s_high, v, NN) + matmul(s_low, v, NN)
 
 
-def attention_rest(q_ref, gain_ref, rate_ref, len_ref, in_ref, attention_buf, normed_buf):
-    offsets, entering, _ = edge_tables(lax.axis_index("ctx") * ROWS, doc_bounds(len_ref))
-    for h in range(HEADS):
-        cols = pl.ds(h * WIDTH, WIDTH)
-        q = q_ref[:, cols]
-        entry = jnp.where(entering, jnp.exp(-rate_ref[h] * offsets), 0.0)
-        in_high, in_low = split(in_ref[h])
-        attention_buf[:, cols] += entry * (matmul(q, in_high, NN) + matmul(q, in_low, NN))
+def head_columns(head):
+    return pl.ds(pl.multiple_of(head * WIDTH, WIDTH), WIDTH)
+
+
+def attention_head(q_ref, rate_ref, tables, in_ref, attention_buf, head):
+    offsets, entering, _ = tables
+    cols = head_columns(head)
+    q = q_ref[:, cols]
+    entry = jnp.where(entering, jnp.exp(-rate_ref[head] * offsets), 0.0)
+    in_high, in_low = split(in_ref[head])
+    attention_buf[:, cols] += entry * (matmul(q, in_high, NN) + matmul(q, in_low, NN))
+
+
+def norm_part(gain_ref, attention_buf, normed_buf):
     attention = attention_buf[...]
     mean = jnp.mean(attention * attention, axis=-1, keepdims=True)
     normed_buf[...] = (attention * lax.rsqrt(mean + norm_eps) * gain_ref[...]).astype(bf16)
+
+
+def gradient_head(k_ref, v_ref, rate_ref, tables, grad_ref, dk_part, dv_part, dk_ref, dv_ref, head):
+    offsets, _, leaving = tables
+    cols = head_columns(head)
+    k, v = k_ref[:, cols], v_ref[:, cols]
+    leave = jnp.where(leaving, jnp.exp(-rate_ref[head] * (ROWS - offsets)), 0.0)
+    grad_high, grad_low = split(grad_ref[head])
+    dk = leave * (matmul(v, grad_high, NT) + matmul(v, grad_low, NT))
+    dk_ref[:, cols] = (dk_part[:, cols] + dk).astype(bf16)
+    dv = leave * (matmul(k, grad_high, NN) + matmul(k, grad_low, NN))
+    dv_ref[:, cols] = (dv_part[:, cols] + dv).astype(bf16)
+
+
+def hand_over(*refs):
+    for src, dst in zip(refs[:len(refs) // 2], refs[len(refs) // 2:]):
+        dst[...] = src[...]
 
 
 def pair_tables(base, bounds):
@@ -279,26 +305,10 @@
         dv_ref[:, cols] = matmul(s_high, g, TN) + matmul(s_low, g, TN)
 
 
-def gradients_kernel(
-    k_ref, v_ref, rate_ref, len_ref, grad_ref, dq_part, dk_part, dv_part, dq_ref, dk_ref, dv_ref,
-):
-    offsets, _, leaving = edge_tables(lax.axis_index("ctx") * ROWS, doc_bounds(len_ref))
-    dq_ref[...] = dq_part[...]
-    for h in range(HEADS):
-        cols = pl.ds(h * WIDTH, WIDTH)
-        k, v = k_ref[:, cols], v_ref[:, cols]
-        leave = jnp.where(leaving, jnp.exp(-rate_ref[h] * (ROWS - offsets)), 0.0)
-        grad_high, grad_low = split(grad_ref[h])
-        dk = leave * (matmul(v, grad_high, NT) + matmul(v, grad_low, NT))
-        dk_ref[:, cols] = (dk_part[:, cols] + dk).astype(bf16)
-        dv = leave * (matmul(k, grad_high, NN) + matmul(k, grad_low, NN))
-        dv_ref[:, cols] = (dv_part[:, cols] + dv).astype(bf16)
-
-
 def main_kernel(
     scale, q_ref, k_ref, v_ref, g_ref, layer_ref, gain_ref, rate_ref, len_ref,
-    out_ref, grad_ref, dq_ref, dk_ref, dv_ref,
-    state_ref, pull_ref, carry_ref, in_ref, px_ref, pz_ref, attention_buf, normed_buf, cx_buf, ax_buf, x_buf, bx_buf, xz_buf, cz_buf, az_buf, z_buf, bz_buf, zx_buf, c_buf, y_buf,
+    dq_ref, dk_ref, dv_ref, out_ref,
+    grad_ref, dk_part, dv_part, state_ref, pull_ref, carry_ref, in_ref, px_ref, pz_ref, attention_buf, normed_buf, cx_buf, ax_buf, x_buf, bx_buf, xz_buf, cz_buf, az_buf, z_buf, bz_buf, zx_buf, c_buf, y_buf,
     core_send, core_recv, x_send, x_recv, xz_send, xz_recv,
     z_send, z_recv, zx_send, zx_recv, y_send, y_recv, *scratch,
 ):
@@ -342,12 +352,14 @@
     scan.pass_on(0)
     ahead.pass_on(1)
     scan.scatter(FAR)
-    ahead.arrive()
-    attention_rest(q_ref, gain_ref, rate_ref, len_ref, in_ref, attention_buf, normed_buf)
+    tables = edge_tables(ctx * ROWS, doc_bounds(len_ref))
+    ahead.arrive(
+        functools.partial(attention_head, q_ref, rate_ref, tables, in_ref, attention_buf)
+    )
+    norm_part(gain_ref, attention_buf, normed_buf)
 
     def product(block, columns):
-        features = pl.ds(pl.multiple_of(block * WIDTH, WIDTH), WIDTH)
-        return matmul(normed_buf[:, features], layer_ref[:, columns], TN)
+        return matmul(normed_buf[:, head_columns(block)], layer_ref[:, columns], TN)
 
     for h in range(HEADS):
         rows = product(h, slice(XCOLS, None))
@@ -390,7 +402,7 @@
             x_copies += started([send(ax_buf.at[k], x_buf.at[k], (x_send, x_recv), k, at_x(k))])
     scan.totals()
     z_copies = to_z((1, 2)) + z_copies + to_z((6, 7))
-    block_part(q_ref, k_ref, v_ref, g_ref, rate_ref, len_ref, in_ref, dq_ref, dk_ref, dv_ref)
+    block_part(q_ref, k_ref, v_ref, g_ref, rate_ref, len_ref, in_ref, dq_ref, dk_part, dv_part)
     scan.combine()
     scan.half_way(1)
     scan.give_back(DIRECT)
@@ -421,8 +433,10 @@
         send(c_buf.at[lax.rem(y + k, NY)], y_buf.at[k], (y_send, y_recv), k, at_y(k))
         for k in range(1, NY)
     ])
+    scan.arrive(functools.partial(
+        gradient_head, k_ref, v_ref, rate_ref, tables, grad_ref, dk_part, dv_part, dk_ref, dv_ref
+    ))
     out_ref[...] = gather(c_buf[y], y_copies, y_buf) * scale
-    scan.arrive()
     scan.finish()
     ahead.finish()
     for copy in core_copies + x_copies + z_copies + xz_copies + zx_copies + y_copies:
@@ -434,17 +448,19 @@
     scale = 1.0 / math.sqrt(rows * lax.axis_size("dp") * lax.axis_size("ctx"))
     q, k, v, g = (a.reshape(rows, features) for a in (queries, keys, values, out_grad))
     layer = layer_grad.reshape(rows, bucket)
-    states = jax.ShapeDtypeStruct((HEADS, WIDTH, WIDTH), f32)
     zcols = bucket - XCOLS
     dma = pltpu.SemaphoreType.DMA
-    part = jax.ShapeDtypeStruct((rows, features), f32)
     grad_shape = jax.ShapeDtypeStruct((rows, features), bf16)
-    proj_grad, state_grad, *parts = pl.pallas_call(
+    results = (grad_shape,) * 3 + (jax.ShapeDtypeStruct((2, bucket), f32),)
+    parts = pl.pallas_call(
         functools.partial(main_kernel, scale),
-        out_shape=(jax.ShapeDtypeStruct((2, bucket), f32), states, grad_shape, part, part),
+        out_shape=results,
         in_specs=[VMEM_SPEC] * 6 + [SMEM_SPEC] * 2,
-        out_specs=(VMEM_SPEC,) * 5,
+        out_specs=(VMEM_SPEC,) * 4,
         scratch_shapes=[
+            HEADS_BUF,
+            pltpu.VMEM((rows, features), f32),
+            pltpu.VMEM((rows, features), f32),
             HEADS_BUF,
             HEADS_BUF,
             pltpu.VMEM((16, WIDTH), f32),
@@ -465,13 +481,13 @@
         compiler_params=pltpu.CompilerParams(collective_id=0, has_side_effects=True),
         name="main",
     )(q, k, v, g, layer, norm_gain.reshape(1, features), decay_rates, doc_lengths)
-    query_grad, key_grad, value_grad = pl.pallas_call(
-        gradients_kernel,
-        out_shape=(grad_shape,) * 3,
-        in_specs=[VMEM_SPEC] * 2 + [SMEM_SPEC] * 2 + [VMEM_SPEC] * 4,
-        out_specs=(VMEM_SPEC,) * 3,
-        name="gradients",
-    )(k, v, decay_rates, doc_lengths, state_grad, *parts)
+    query_grad, key_grad, value_grad, proj_grad = pl.pallas_call(
+        hand_over,
+        out_shape=results,
+        in_specs=[VMEM_SPEC] * 4,
+        out_specs=(VMEM_SPEC,) * 4,
+        name="results",
+    )(*parts)
     shape_out = (1, rows, features)
     return (
         query_grad.reshape(shape_out),

time: 90.5 us -> 87.6 us (0.968)
  Pallas kernels: 88 us -> 86.5 us
  local copies, waits for them, and re-layouts: 1.28 us -> 0 us
    pallas_call x2, Pallas kernels: 88 us -> 86.5 us  [the longest x1 84.5 us: on_device(): pl.pallas_call(functools.partial(main_kernel, scale), out_shape=results,...]
    unnamed x3 -> x0, local copies, waits for them, and re-layouts: 1.28 us -> none
where the time goes in v6:
time: 87.6 us; the launch traced here: 87.2 us
  Pallas kernels  86.5 us (99%)
    pallas_call x1, Pallas kernels, on_device(): pl.pallas_call(functools.partial(main_kernel, scale), out_shape=results,...  84.5 us
    pallas_call x1, Pallas kernels, on_device(): pl.pallas_call(hand_over, out_shape=results, in_specs=[VMEM_SPEC] * 4, ou...  2.01 us

profile of v6, /device:TPU:1, one launch (start us, length us, event | category | flops | bytes accessed | tf_op | source)
XLA Modules:
  0.0 87.2 jit_solution(8790644106291600594)
XLA Ops:
  0.6 84.5 %main.1 = (bf16[128,1024]{1,0:T(8,128)(2,1)}, bf16[128,1024]{1,0:T(8,128)(2,1)}, bf16[128,1024]{1,0:T(8,128)(2,1)}, f32[2,768]{1,0:T(2,128)}) custom-call(bf16[128,1024]{1,0:T(8,128)(2,1)} %bitcast.9, bf16[128,1024]{1,0:T(8,128)(2,1)} %bitcast.10, bf16[128,1024]{1,0:T(8,128)(2,1)} %bitcast.11, bf16[128,1024]{1,0:T(8,128)(2,1)} %bitcast.12, ...), custom_call_target="tpu_custom_call" | custom-call | tf_op jit(solution)/shard_map/main/pallas_call | solution.py:455
  85.2 2.0 %results.1 = (bf16[128,1024]{1,0:T(8,128)(2,1)}, bf16[128,1024]{1,0:T(8,128)(2,1)}, bf16[128,1024]{1,0:T(8,128)(2,1)}, f32[2,768]{1,0:T(2,128)}) custom-call(bf16[128,1024]{1,0:T(8,128)(2,1)} %get-tuple-element.12.refs_0_, bf16[128,1024]{1,0:T(8,128)(2,1)} %get-tuple-element.13.refs_1_, bf16[128,1024]{1,0:T(8,128)(2,1)} %get-tuple-element.14.refs_2_, ...), custom_call_target="tpu_custom_call" | custom-call | tf_op jit(solution)/shard_map/results/pallas_call | solution.py:484

commit v7 on v6

--- a/solution.py
+++ b/solution.py
@@ -105,18 +105,13 @@
     return copies
 
 
-HALF = WIDTH // 2
-SIDES = ((1, 3, 0), (NY - 1, NY - 3, HALF))
-
-
 class Scan:
     def __init__(self, step, src, carry, result, scratch):
         self.step, self.src, self.carry_ref, self.result = step, src, carry, result
-        self.buf, self.back, self.total, self.group, self.relay = scratch[:5]
-        sems = [scratch[i:i + 2] for i in range(5, 15, 2)]
-        self.out_sems, self.back_sems, self.near_sems, self.far_sems, self.group_sems = sems
+        self.buf, self.back, self.total, self.group = scratch[:4]
+        self.out_sems, self.back_sems, self.group_sems = scratch[4:6], scratch[6:8], scratch[8:10]
         self.dp, _, self.z, self.y = place()
-        self.out_copies, self.back_copies, self.relay_copies = [], [], []
+        self.out_copies, self.back_copies = [], []
         self.order = range(NY) if step > 0 else range(NY - 1, -1, -1)
 
     def around(self, k):
@@ -130,32 +125,6 @@
 
     def block(self, j):
         return self.buf[lax.rem(self.y - j + NY, NY)]
-
-    def half_way(self, phase):
-        src = (self.src, self.back)[phase].at[self.around(NY // 2)]
-        for side, (near, _, row) in enumerate(SIDES):
-            at = 2 * phase + side
-            self.relay_copies += started([
-                send(src.at[pl.ds(row, HALF)], self.relay.at[at], self.near_sems, at, self.at_y(near))
-            ])
-
-    def pass_on(self, phase):
-        for copy in self.relay_copies[-2:]:
-            copy.wait_recv()
-        for side, (near, far, row) in enumerate(SIDES):
-            at = 2 * phase + side
-            slot = self.result.at[self.around(NY - near)] if phase else self.buf.at[NY // 2]
-            self.relay_copies += started([
-                send(self.relay.at[at], slot.at[pl.ds(row, HALF)], self.far_sems, at, self.at_y(far))
-            ])
-
-    def half_way_arrived(self, phase):
-        for side, (_, far, row) in enumerate(SIDES):
-            at = 2 * phase + side
-            slot = self.result.at[self.around(NY // 2)] if phase else self.buf.at[NY // 2]
-            send(
-                self.relay.at[at], slot.at[pl.ds(row, HALF)], self.far_sems, at, self.at_y(far)
-            ).wait_recv()
 
     def scatter(self, offsets):
         self.out_copies += started([
@@ -175,7 +144,6 @@
         self.buf[0] = self.src[self.y]
         for copy in self.out_copies:
             copy.wait_recv()
-        self.half_way_arrived(0)
         total = jnp.zeros((WIDTH, WIDTH), f32)
         for j in self.order:
             total = self.carry(j) * total + self.block(j)
@@ -211,23 +179,20 @@
                 self.back.at[0], self.result.at[self.around(NY - k)], self.back_sems, k, self.at_y(k)
             ).wait_recv()
             use(self.around(NY - k))
-        self.half_way_arrived(1)
-        use(self.around(NY // 2))
 
     def finish(self):
         for far in (1, 2):
             pl.when(self.has(self.step * far))(lambda far=far: self.group_copy(far).wait_send())
-        for copy in self.out_copies + self.back_copies + self.relay_copies:
+        for copy in self.out_copies + self.back_copies:
             copy.wait_send()
 
 
-FAR, NEAR = (3, 5), (2, 6, 1, 7)
+FAR, NEAR = (4, 3, 5), (2, 6, 1, 7)
 DIRECT = FAR + NEAR
 HEADS_BUF = pltpu.VMEM((HEADS, WIDTH, WIDTH), f32)
 SCAN_SCRATCH = [
     HEADS_BUF, HEADS_BUF, pltpu.VMEM((WIDTH, WIDTH), f32), pltpu.VMEM((2, WIDTH, WIDTH), f32),
-    pltpu.VMEM((4, HALF, WIDTH), f32),
-] + [pltpu.SemaphoreType.DMA((NY,))] * 4 + [pltpu.SemaphoreType.DMA((4,))] * 4 + [pltpu.SemaphoreType.DMA((2,))] * 2
+] + [pltpu.SemaphoreType.DMA((NY,))] * 4 + [pltpu.SemaphoreType.DMA((2,))] * 2
 
 
 def attention_block(q_ref, k_ref, v_ref, rate_ref, len_ref, attention_buf):
@@ -327,8 +292,8 @@
     def at_y(k):
         return (dp, ctx - y + lax.rem(y + k, NY))
 
-    ahead = Scan(1, state_ref, carry_ref, in_ref, scratch[:15])
-    scan = Scan(-1, pull_ref, carry_ref, grad_ref, scratch[15:])
+    ahead = Scan(1, state_ref, carry_ref, in_ref, scratch[:10])
+    scan = Scan(-1, pull_ref, carry_ref, grad_ref, scratch[10:])
     partners = (
         [twin] + [at_x(k) for k in range(1, NX)] + [at_z(k) for k in range(1, NZ)]
         + [at_y(k) for k in range(1, NY)]
@@ -338,19 +303,13 @@
         pl.semaphore_signal(barrier, inc=1, device_id=device, device_id_type=MESH)
     state_part(k_ref, v_ref, rate_ref, len_ref, state_ref, carry_ref)
     pl.semaphore_wait(barrier, len(partners))
-    ahead.half_way(0)
     ahead.scatter(DIRECT)
     pull_part(q_ref, g_ref, rate_ref, len_ref, pull_ref)
-    ahead.pass_on(0)
     attention_block(q_ref, k_ref, v_ref, rate_ref, len_ref, attention_buf)
     ahead.totals()
-    scan.half_way(0)
     scan.scatter(NEAR)
     ahead.combine()
-    ahead.half_way(1)
     ahead.give_back(DIRECT)
-    scan.pass_on(0)
-    ahead.pass_on(1)
     scan.scatter(FAR)
     tables = edge_tables(ctx * ROWS, doc_bounds(len_ref))
     ahead.arrive(
@@ -404,7 +363,6 @@
     z_copies = to_z((1, 2)) + z_copies + to_z((6, 7))
     block_part(q_ref, k_ref, v_ref, g_ref, rate_ref, len_ref, in_ref, dq_ref, dk_part, dv_part)
     scan.combine()
-    scan.half_way(1)
     scan.give_back(DIRECT)
 
     def gather(total, copies, buf):
@@ -418,7 +376,6 @@
         send(bx_buf.at[lax.rem(z + k, NZ)], xz_buf.at[k], (xz_send, xz_recv), k, at_z(k))
         for k in range(1, NZ)
     ])
-    scan.pass_on(1)
     bz_buf[...] = gather(az_buf[z], z_copies, z_buf)
     zx_copies = started([
         send(bz_buf.at[lax.rem(x + k, NX)], zx_buf.at[k], (zx_send, zx_recv), k, at_x(k))

time: 87.6 us -> 86.6 us (0.989)
  no operation moved by 1% of the time
where the time goes in v7:
time: 86.6 us; the launch traced here: 86.4 us
  Pallas kernels  85.8 us (99%)
    pallas_call x1, Pallas kernels, on_device(): pl.pallas_call(functools.partial(main_kernel, scale), out_shape=results,...  83.8 us
    pallas_call x1, Pallas kernels, on_device(): pl.pallas_call(hand_over, out_shape=results, in_specs=[VMEM_SPEC] * 4, ou...  2.01 us

profile of v7, /device:TPU:1, one launch (start us, length us, event | category | flops | bytes accessed | tf_op | source)
XLA Modules:
  0.0 86.4 jit_solution(17580529418770055495)
XLA Ops:
  0.6 83.8 %main.1 = (bf16[128,1024]{1,0:T(8,128)(2,1)}, bf16[128,1024]{1,0:T(8,128)(2,1)}, bf16[128,1024]{1,0:T(8,128)(2,1)}, f32[2,768]{1,0:T(2,128)}) custom-call(bf16[128,1024]{1,0:T(8,128)(2,1)} %bitcast.9, bf16[128,1024]{1,0:T(8,128)(2,1)} %bitcast.10, bf16[128,1024]{1,0:T(8,128)(2,1)} %bitcast.11, bf16[128,1024]{1,0:T(8,128)(2,1)} %bitcast.12, ...), custom_call_target="tpu_custom_call" | custom-call | tf_op jit(solution)/shard_map/main/pallas_call | solution.py:412
  84.4 2.0 %results.1 = (bf16[128,1024]{1,0:T(8,128)(2,1)}, bf16[128,1024]{1,0:T(8,128)(2,1)}, bf16[128,1024]{1,0:T(8,128)(2,1)}, f32[2,768]{1,0:T(2,128)}) custom-call(bf16[128,1024]{1,0:T(8,128)(2,1)} %get-tuple-element.12.refs_0_, bf16[128,1024]{1,0:T(8,128)(2,1)} %get-tuple-element.13.refs_1_, bf16[128,1024]{1,0:T(8,128)(2,1)} %get-tuple-element.14.refs_2_, ...), custom_call_target="tpu_custom_call" | custom-call | tf_op jit(solution)/shard_map/results/pallas_call | solution.py:441

commit v8 on v7

--- a/solution.py
+++ b/solution.py
@@ -102,6 +102,13 @@
 def started(copies):
     for copy in copies:
         copy.start()
+    return copies
+
+
+def started_far_first(copies):
+    count = len(copies) + 1
+    for k in sorted(range(1, count), key=lambda k: -min(k, count - k)):
+        copies[k - 1].start()
     return copies
 
 
@@ -372,12 +379,12 @@
         return total
 
     bx_buf[...] = gather(ax_buf[0], x_copies, x_buf).reshape(bx_buf.shape)
-    xz_copies = started([
+    xz_copies = started_far_first([
         send(bx_buf.at[lax.rem(z + k, NZ)], xz_buf.at[k], (xz_send, xz_recv), k, at_z(k))
         for k in range(1, NZ)
     ])
     bz_buf[...] = gather(az_buf[z], z_copies, z_buf)
-    zx_copies = started([
+    zx_copies = started_far_first([
         send(bz_buf.at[lax.rem(x + k, NX)], zx_buf.at[k], (zx_send, zx_recv), k, at_x(k))
         for k in range(1, NX)
     ])
@@ -386,7 +393,7 @@
     for j in range(NY):
         c_buf[j, :, :XCOLS] = left[2 * j:2 * j + 2, :]
         c_buf[j, :, XCOLS:] = right[2 * j:2 * j + 2, :]
-    y_copies = started([
+    y_copies = started_far_first([
         send(c_buf.at[lax.rem(y + k, NY)], y_buf.at[k], (y_send, y_recv), k, at_y(k))
         for k in range(1, NY)
     ])

time: 86.6 us -> 86.3 us (level)
  no operation moved by 1% of the time
where the time goes in v8:
time: 86.3 us; the launch traced here: 86.1 us
  Pallas kernels  85.5 us (99%)
    pallas_call x1, Pallas kernels, on_device(): pl.pallas_call(functools.partial(main_kernel, scale), out_shape=results,...  83.5 us
    pallas_call x1, Pallas kernels, on_device(): pl.pallas_call(hand_over, out_shape=results, in_specs=[VMEM_SPEC] * 4, ou...  2.01 us

profile of v8, /device:TPU:1, one launch (start us, length us, event | category | flops | bytes accessed | tf_op | source)
XLA Modules:
  0.0 86.1 jit_solution(118213413581139271)
XLA Ops:
  0.6 83.5 %main.1 = (bf16[128,1024]{1,0:T(8,128)(2,1)}, bf16[128,1024]{1,0:T(8,128)(2,1)}, bf16[128,1024]{1,0:T(8,128)(2,1)}, f32[2,768]{1,0:T(2,128)}) custom-call(bf16[128,1024]{1,0:T(8,128)(2,1)} %bitcast.9, bf16[128,1024]{1,0:T(8,128)(2,1)} %bitcast.10, bf16[128,1024]{1,0:T(8,128)(2,1)} %bitcast.11, bf16[128,1024]{1,0:T(8,128)(2,1)} %bitcast.12, ...), custom_call_target="tpu_custom_call" | custom-call | tf_op jit(solution)/shard_map/main/pallas_call | solution.py:419
  84.1 2.0 %results.1 = (bf16[128,1024]{1,0:T(8,128)(2,1)}, bf16[128,1024]{1,0:T(8,128)(2,1)}, bf16[128,1024]{1,0:T(8,128)(2,1)}, f32[2,768]{1,0:T(2,128)}) custom-call(bf16[128,1024]{1,0:T(8,128)(2,1)} %get-tuple-element.12.refs_0_, bf16[128,1024]{1,0:T(8,128)(2,1)} %get-tuple-element.13.refs_1_, bf16[128,1024]{1,0:T(8,128)(2,1)} %get-tuple-element.14.refs_2_, ...), custom_call_target="tpu_custom_call" | custom-call | tf_op jit(solution)/shard_map/results/pallas_call | solution.py:448
